TPU v7x, 256 devices: a whole 4x4x8 slice. The times are simulated.
256 devices in a mesh: slab: 4 (over x), range: 64 (over y, z, core).
Axes of the slice: x: 4, y: 4, z: 8, core: 2. Of those that a mesh axis runs over, the one named last changes fastest.
Arguments:
- features: bfloat16 [512, 512, 128], P(('slab', 'range')), may hold values from -54 to 54
- neighbours: int32 [512, 26], P(('slab', 'range')), may hold values from -1 to 9, as said below
- keep_mask: int32 [512, 8], P(('slab', 'range')), may hold values from 0 to 1, as said below
- owner: int32 [512, 8], P(('slab', 'range')), may hold values from 0 to 63, as said below
- norm_gain: float32 [4, 128], replicated, may hold values from 0.1 to 1.9
- norm_shift: float32 [4, 128], replicated, may hold values from -3 to 3
- conv_weights: bfloat16 [4, 27, 128, 128], replicated, may hold values from -0.109375 to 0.109375
- up_weight: bfloat16 [128, 512], replicated, may hold values from -0.5 to 0.5
Outputs:
- children: bfloat16 [32768, 64, 512], P(('slab', 'range'))
Inputs may be any that keep to these rules, and one draw needn't show every extreme that they name: `neighbours`: entries are -1 (no neighbour) or q * 2 + slot as in the first step; directions whose first nonzero component is -1 use q in 0, 1, 3, the others q in 0, 2, 4; q = 3 only where dx = -1 and q = 4 only where dx = +1; no entry names a device outside the mesh. `keep_mask`: 1 keeps the child. Among the kept children of one device at most 2 have the same owner, and in every slab group one owner receives exactly 2 kept children from every device of the group.
All inputs are finite; a program needn't handle non-finite values.
Results may differ from a plain program's by a relative error of at most 0.013.
Values may be sent and summed in bfloat16 or wider, within the bound.
No kernel may reach another device: no remote copies, remote signals or barrier semaphores. Data moves between devices by JAX's collectives and lax.ppermute only.
A program may use at most 128 MiB of HBM per device.

v0:
```python
import functools

import jax
import jax.numpy as jnp
from jax import lax
from jax.experimental import pallas as pl
from jax.experimental.pallas import tpu as pltpu
from jax.sharding import PartitionSpec as P

EDGE = 8
CH = 128
BRICKS = 2
VOX = EDGE**3
OCT = 64
PITCH = 24
FACE = EDGE * EDGE
DIRECTIONS = [
    (dx, dy, dz)
    for dx in (-1, 0, 1)
    for dy in (-1, 0, 1)
    for dz in (-1, 0, 1)
    if (dx, dy, dz) != (0, 0, 0)
]
OWN_HI, OWN_LO, CORE, RANGE, SLAB_A, SLAB_B, ZERO = 0, 6, 12, 18, 24, 26, 28
FACES = 29

VMEM = pl.BlockSpec(memory_space=pltpu.VMEM)
SMEM = pl.BlockSpec(memory_space=pltpu.SMEM)
ANY = pl.BlockSpec(memory_space=pl.ANY)


def group_sum(rows):
    lane = lax.broadcasted_iota(jnp.int32, rows.shape, 1)
    pair = jnp.where(lane % 2 == 0, pltpu.roll(rows, CH - 1, 1), pltpu.roll(rows, 1, 1))
    rows = rows + pair
    pair = jnp.where(lane % 4 < 2, pltpu.roll(rows, CH - 2, 1), pltpu.roll(rows, 2, 1))
    return jnp.sum(rows + pair, axis=0, keepdims=True)


def normalize(load, gain, shift):
    size = VOX * 4.0
    mean = group_sum(jnp.sum(load(), axis=0)) / size
    centred = load() - mean
    spread = group_sum(jnp.sum(centred * centred, axis=0)) / size
    scale = lax.rsqrt(spread + 1e-6) * gain
    w = (load() - mean) * scale + shift
    return w * (0.5 + 0.5 * jnp.tanh(0.5 * w))


def emit_active(load, b, gain, shift, info, act_s, act, sends):
    value = normalize(load, gain, shift)
    act_s[pl.ds(b * VOX, VOX)] = value.reshape(VOX, CH)
    act[b] = value.reshape(VOX, CH).astype(jnp.bfloat16)
    last, first, to_core, to_range, to_a, to_b = sends
    base = b * VOX
    for x in range(EDGE):
        rows = pl.ds(x * EDGE, EDGE)
        for side, plane in ((7, last), (0, first)):
            plane[0, b, rows] = act_s[pl.ds(base + side * 64 + x * 8, 8)].astype(jnp.bfloat16)
            plane[1, b, rows] = act_s[pl.ds(base + x * 64 + side * 8, 8)].astype(jnp.bfloat16)
            plane[2, b, rows] = act_s[pl.ds(base + x * 64 + side, 8, stride=8)].astype(jnp.bfloat16)


def choose_sends(info, sends):
    last, first, to_core, to_range, to_a, to_b = sends

    def route(flag, yes, no):
        @pl.when(flag == 0)
        def _():
            yes[...] = last[...] if yes.shape[0] == 3 else last[0]
            no[...] = first[...] if no.shape[0] == 3 else first[0]

        @pl.when(flag != 0)
        def _():
            yes[...] = first[...] if yes.shape[0] == 3 else first[0]
            no[...] = last[...] if no.shape[0] == 3 else last[0]

    route(info[0], to_core, to_range)
    route(info[1], to_a, to_b)


def start_kernel(
    info, features, neighbours, kept, owner, gain, shift,
    act, last, first, to_core, to_range, to_a, to_b, faces, slots, act_s,
):
    sends = (last, first, to_core, to_range, to_a, to_b)
    for b in range(BRICKS):
        load = lambda b=b: features[b].astype(jnp.float32).reshape(OCT, EDGE, CH)
        emit_active(load, b, gain[0:1], shift[0:1], info, act_s, act, sends)
    choose_sends(info, sends)
    odd_range, odd_slab = info[0], info[1]
    below = jnp.where(odd_range == 1, CORE, RANGE)
    above = jnp.where(odd_range == 1, RANGE, CORE)
    under = jnp.where(odd_slab == 1, SLAB_A, SLAB_B)
    over = jnp.where(odd_slab == 1, SLAB_B, SLAB_A)
    for b in range(BRICKS):
        for k, offsets in enumerate(DIRECTIONS):
            axis = [a for a in range(3) if offsets[a] != 0][0]
            negative = offsets[axis] < 0
            entry = neighbours[b, k]
            source = entry // BRICKS
            own, side, slab = (OWN_HI, below, under) if negative else (OWN_LO, above, over)
            near = jnp.where(source == 0, own, side) + axis * BRICKS
            face = jnp.where(source > 2, slab, near) + entry % BRICKS
            face = jnp.where(entry < 0, ZERO, jnp.clip(face, 0, ZERO))
            faces[b, k] = face * FACE
    owners = [owner[c // 8, c % 8] for c in range(8 * BRICKS)]
    keeps = [kept[c // 8, c % 8] for c in range(8 * BRICKS)]
    for c in range(8 * BRICKS):
        rank = jnp.int32(0)
        for e in range(c):
            same = (owners[e] == owners[c]) & (keeps[e] == 1)
            rank = rank + jnp.where(same, 1, 0)
        slot = jnp.clip(owners[c] * 2 + jnp.minimum(rank, 1), 0, 127)
        slots[c] = jnp.where(keeps[c] == 1, slot, -1)


def assemble(act, faces, planes, table, field, window):
    row = 0
    for plane in planes:
        whole = plane[...].astype(jnp.float32)
        count = whole.size // CH
        table[pl.ds(row, count)] = whole.reshape(count, CH)
        row += count
    table[pl.ds(ZERO * FACE, FACE)] = jnp.zeros((FACE, CH), jnp.float32)

    def cell(x, y, b):
        return ((x * 10 + y) * BRICKS + b) * PITCH

    for b in range(BRICKS):
        for x in range(EDGE):
            for y in range(EDGE):
                tile = act[b, pl.ds((x * 8 + y) * 8, 8)].astype(jnp.float32)
                field[pl.ds(cell(x + 1, y + 1, b) + 8, 8)] = tile
    for b in range(BRICKS):
        for k, (dx, dy, dz) in enumerate(DIRECTIONS):
            base = pl.multiple_of(faces[b, k], FACE)
            cut = lambda d: 7 if d < 0 else 0
            put = lambda d: 0 if d < 0 else 9
            deep = 7 if dz < 0 else 16
            if dx != 0:
                px = put(dx)
                ys = range(EDGE) if dy == 0 else [None]
                if dz == 0:
                    for y in ys:
                        sy, py = (y, y + 1) if dy == 0 else (cut(dy), put(dy))
                        field[pl.ds(cell(px, py, b) + 8, 8)] = table[pl.ds(base + sy * 8, 8)]
                elif dy == 0:
                    column = table[pl.ds(base + cut(dz), 8, stride=8)]
                    field[pl.ds(cell(px, 1, b) + deep, 8, stride=BRICKS * PITCH)] = column
                else:
                    corner = table[pl.ds(base + cut(dy) * 8 + cut(dz), 1)]
                    field[pl.ds(cell(px, put(dy), b) + deep, 1)] = corner
            elif dy != 0:
                py = put(dy)
                if dz == 0:
                    for x in range(EDGE):
                        field[pl.ds(cell(x + 1, py, b) + 8, 8)] = table[pl.ds(base + x * 8, 8)]
                else:
                    column = table[pl.ds(base + cut(dz), 8, stride=8)]
                    field[pl.ds(cell(1, py, b) + deep, 8, stride=10 * BRICKS * PITCH)] = column
            else:
                for x in range(EDGE):
                    rows = table[pl.ds(base + x * 8, 8)]
                    field[pl.ds(cell(x + 1, 1, b) + deep, 8, stride=BRICKS * PITCH)] = rows
    for x in range(10):
        for y in range(10):
            for w in range(3):
                tile = jnp.concatenate(
                    [field[pl.ds(cell(x, y, b) + 7 + w, 8)] for b in range(BRICKS)], axis=0
                )
                window[x, y, :, w * CH : (w + 1) * CH] = tile.astype(jnp.bfloat16)


def convolve(window, weights, total):
    for p in range(3):
        rows = jnp.concatenate([window[p : p + 8, t : t + 8] for t in range(3)], axis=-1)
        part = jnp.dot(
            rows.reshape(BRICKS * VOX, 9 * CH),
            weights[p * 9 * CH : (p + 1) * 9 * CH],
            preferred_element_type=jnp.float32,
        ).reshape(OCT, BRICKS, EDGE, CH)
        if p == 0:
            total[...] = part
        else:
            total[...] += part


def conv_kernel(
    step, info, faces, act, last, first, core, rng, slab_a, slab_b, weights_hbm, gain, shift, *rest,
):
    rest = list(rest)
    state = rest.pop(0) if step % 2 else None
    slots = rest.pop(0) if step == 3 else None
    if step == 3:
        packed = rest.pop(0)
    else:
        act_out = rest.pop(0)
        sends = [rest.pop(0) for _ in range(6)]
        state_out = rest.pop(0) if step == 1 else None
    table, field, window, weights, total, act_s, sem = rest
    copy = pltpu.make_async_copy(weights_hbm.at[step], weights, sem)
    copy.start()
    assemble(act, faces, (last, first, core, rng, slab_a, slab_b), table, field, window)
    if step == 3:
        packed[...] = jnp.zeros(packed.shape, packed.dtype)
    copy.wait()
    convolve(window, weights, total)
    for b in range(BRICKS):
        if step % 2:
            value = total[:, b] + state[b].astype(jnp.float32).reshape(OCT, EDGE, CH)
            value = value.astype(jnp.bfloat16)
            if step == 1:
                state_out[b] = value.reshape(VOX, CH)
            total[:, b] = value.astype(jnp.float32)
        else:
            total[:, b] = total[:, b].astype(jnp.bfloat16).astype(jnp.float32)
        if step < 3:
            load = lambda b=b: total[:, b]
            emit_active(load, b, gain[step + 1 : step + 2], shift[step + 1 : step + 2], info, act_s, act_out, sends)
    if step < 3:
        choose_sends(info, sends)
        return
    low = lax.broadcasted_iota(jnp.int32, (4, 2, 8, CH), 2) < 4
    for b in range(BRICKS):
        for ox in range(2):
            for oy in range(2):
                tiles = total[pl.ds(ox * 32, 32), b].reshape(4, 8, EDGE, CH)
                tiles = tiles[:, oy * 4 : oy * 4 + 4].reshape(4, 2, 2, EDGE, CH)
                even, odd = tiles[:, :, 0], tiles[:, :, 1]
                turn = lambda v: pltpu.roll(v.reshape(8, EDGE, CH), 4, 1).reshape(4, 2, EDGE, CH)
                for oz in range(2):
                    block = jnp.where(low, even, turn(odd)) if oz == 0 else jnp.where(low, turn(even), odd)
                    child = b * 8 + (ox * 2 + oy) * 2 + oz
                    block = block.reshape(OCT, CH).astype(jnp.bfloat16)
                    slot = slots[child]

                    @pl.when(slot >= 0)
                    def _(slot=slot, block=block):
                        packed[slot] = block


def grow_kernel(octants, up, out):
    rows = octants[...].reshape(-1, CH)
    grown = jnp.dot(rows, up[...], preferred_element_type=jnp.float32)
    out[...] = grown.astype(jnp.bfloat16).reshape(out.shape)


def bf16(*shape):
    return jax.ShapeDtypeStruct(shape, jnp.bfloat16)


def swap(block, axis, odd):
    count = lax.axis_size(axis)
    route = []
    for i in range(count):
        j = (i ^ 1) if not odd else (i + 1 if i % 2 else i - 1)
        if 0 <= j < count:
            route.append((i, j))
    return lax.ppermute(block, axis, route)


def exchange(sends):
    last, first, to_core, to_range, to_a, to_b = sends
    return (
        last,
        first,
        swap(to_core, "range", False),
        swap(to_range, "range", True),
        swap(to_a, "slab", False),
        swap(to_b, "slab", True),
    )


SENDS = [
    bf16(3, BRICKS, FACE, CH),
    bf16(3, BRICKS, FACE, CH),
    bf16(3, BRICKS, FACE, CH),
    bf16(3, BRICKS, FACE, CH),
    bf16(BRICKS, FACE, CH),
    bf16(BRICKS, FACE, CH),
]
LIMIT = 48 * 1024 * 1024


def shards(features, neighbours, keep_mask, owner, norm_gain, norm_shift, conv_weights, up_weight):
    info = jnp.stack([lax.axis_index("range") % 2, lax.axis_index("slab") % 2]).astype(jnp.int32)
    act_s = pltpu.VMEM((BRICKS * VOX, CH), jnp.float32)
    act, *sends, faces, slots = pl.pallas_call(
        start_kernel,
        out_shape=[bf16(BRICKS, VOX, CH), *SENDS, jax.ShapeDtypeStruct((BRICKS, 26), jnp.int32),
                   jax.ShapeDtypeStruct((8 * BRICKS,), jnp.int32)],
        in_specs=[SMEM, VMEM, SMEM, SMEM, SMEM, VMEM, VMEM],
        out_specs=[VMEM] * 7 + [SMEM, SMEM],
        scratch_shapes=[act_s],
        name="start",
    )(info, features, neighbours, keep_mask, owner, norm_gain, norm_shift)
    weights = conv_weights.reshape(4, 27 * CH, CH)
    state = features
    for step in range(4):
        planes = exchange(sends)
        inputs = [info, faces, act, *planes, weights, norm_gain, norm_shift]
        in_specs = [SMEM, SMEM] + [VMEM] * 7 + [ANY, VMEM, VMEM]
        if step % 2:
            inputs.append(state)
            in_specs.append(VMEM)
        if step == 3:
            inputs.append(slots)
            in_specs.append(SMEM)
            outs = [bf16(128, OCT, CH)]
        else:
            outs = [bf16(BRICKS, VOX, CH), *SENDS]
            if step == 1:
                outs.append(bf16(BRICKS, VOX, CH))
        result = pl.pallas_call(
            functools.partial(conv_kernel, step),
            out_shape=outs,
            in_specs=in_specs,
            out_specs=[VMEM] * len(outs),
            scratch_shapes=[
                pltpu.VMEM((FACES * FACE, CH), jnp.float32),
                pltpu.VMEM((100 * BRICKS * PITCH, CH), jnp.float32),
                pltpu.VMEM((10, 10, BRICKS * EDGE, 3 * CH), jnp.bfloat16),
                pltpu.VMEM((27 * CH, CH), jnp.bfloat16),
                pltpu.VMEM((OCT, BRICKS, EDGE, CH), jnp.float32),
                act_s,
                pltpu.SemaphoreType.DMA,
            ],
            compiler_params=pltpu.CompilerParams(vmem_limit_bytes=LIMIT),
            name=f"conv{step}",
        )(*inputs)
        if step < 3:
            act, sends = result[0], result[1:7]
            if step == 1:
                state = result[7]
    arrived = lax.all_to_all(result[0], "range", split_axis=0, concat_axis=0, tiled=True)
    slab = 8
    return pl.pallas_call(
        grow_kernel,
        grid=(128 // slab,),
        out_shape=bf16(128, OCT, 4 * CH),
        in_specs=[
            pl.BlockSpec((slab, OCT, CH), lambda i: (i, 0, 0)),
            pl.BlockSpec((CH, 4 * CH), lambda i: (0, 0)),
        ],
        out_specs=pl.BlockSpec((slab, OCT, 4 * CH), lambda i: (i, 0, 0)),
        name="grow",
    )(arrived, up_weight)


def solution(mesh):
    split = P(("slab", "range"))
    return jax.shard_map(
        shards,
        mesh=mesh,
        in_specs=(split, split, split, split, P(), P(), P(), P()),
        out_specs=split,
        check_vma=False,
    )
```

profile of v0, /device:TPU:5, one launch (start us, length us, event | category | flops | bytes accessed | tf_op | source)
XLA Modules:
  0.0 139.0 jit_solution(3991633323089686159)
XLA Ops:
  0.0 0.6 pad_add_fusion.info
  0.6 2.9 %start.1 = (bf16[2,512,128]{2,1,0:T(8,128)(2,1)}, bf16[3,2,64,128]{3,2,1,0:T(8,128)(2,1)}, bf16[3,2,64,128]{3,2,1,0:T(8,128)(2,1)}, bf16[3,2,64,128]{3,2,1,0:T(8...) custom-call(s32[2]{0:T(128)} %pad_add_fusion.info, ...), custom_call_target="tpu_custom_call" | custom-call | tf_op jit(solution)/shard_map/start/pallas_call | solution.py:289
  3.5 0.8 collective-permute-start
  4.2 3.4 %collective-permute-start.1 = (bf16[3,2,64,128]{3,2,1,0:T(8,128)(2,1)}, bf16[3,2,64,128]{3,2,1,0:T(8,128)(2,1)S(1)}, u32[]{:S(2)}, u32[]{:S(2)}) collective-permute-start(bf16[3,2,64,128]{3,2,1,0:T(8,128)(2,1)} %get-tuple-element.41), channel_id=1, source_target_pairs={{1,2},{2,1},{3,4},{4,3},{5,6},{6,5},{7,8},{8,7},{9,10},{10,9},{11,... | collective-permute-start | bytes 294920 | tf_op jit(solution)/shard_map/ppermute | solution.py:260
  7.7 1.0 collective-permute-start.2
  8.7 1.9 %collective-permute-start.3 = (bf16[2,64,128]{2,1,0:T(8,128)(2,1)}, bf16[2,64,128]{2,1,0:T(8,128)(2,1)S(1)}, u32[]{:S(2)}, u32[]{:S(2)}) collective-permute-start(bf16[2,64,128]{2,1,0:T(8,128)(2,1)} %get-tuple-element.43), channel_id=1, source_target_pairs={{64,128},{128,64},{65,129},{129,65},{66,130},{130,66},{67,131},{13... | collective-permute-start | bytes 98312 | tf_op jit(solution)/shard_map/ppermute | solution.py:260
  10.6 0.1 collective-permute-done.2.slab_a
  10.7 2.8 %collective-permute-done.3.slab_b = bf16[2,64,128]{2,1,0:T(8,128)(2,1)S(1)} collective-permute-done((bf16[2,64,128]{2,1,0:T(8,128)(2,1)}, bf16[2,64,128]{2,1,0:T(8,128)(2,1)S(1)}, u32[]{:S(2)}, u32[]{:S(2)}) %collective-permute-start.3) | collective-permute-done | bytes 32800 | tf_op jit(solution)/shard_map/ppermute | solution.py:260
  13.5 0.0 collective-permute-done.core
  13.5 0.0 collective-permute-done.1.rng
  13.5 2.0 %copy-done = bf16[4,27,128,128]{3,2,1,0:T(8,128)(2,1)S(1)} copy-done((bf16[4,27,128,128]{3,2,1,0:T(8,128)(2,1)S(1)}, bf16[4,27,128,128]{3,2,1,0:T(8,128)(2,1)}, u32[]{:S(2)}) %copy-start) | copy-done | bytes 3538968
  15.5 0.9 copy-done.3
  16.5 0.9 copy-done.4
  17.4 0.9 copy-done.5
  18.3 0.7 copy-done.6
  19.0 0.7 copy-done.7
  19.6 0.7 copy-done.8
  20.3 0.6 copy-done.10
  20.9 3.7 %conv0.1 = (bf16[2,512,128]{2,1,0:T(8,128)(2,1)S(1)}, bf16[3,2,64,128]{3,2,1,0:T(8,128)(2,1)S(1)}, bf16[3,2,64,128]{3,2,1,0:T(8,128)(2,1)S(1)}, bf16[3,2,64,128]...) custom-call(s32[2]{0:T(128)S(1)} %copy-done.10, ...), custom_call_target="tpu_custom_call" | custom-call | tf_op jit(solution)/shard_map/conv0/pallas_call | solution.py:315
  24.6 0.1 collective-permute-start.4
  24.7 3.9 %collective-permute-start.5 = (bf16[3,2,64,128]{3,2,1,0:T(8,128)(2,1)S(1)}, bf16[3,2,64,128]{3,2,1,0:T(8,128)(2,1)S(1)}, u32[]{:S(2)}, u32[]{:S(2)}) collective-permute-start(bf16[3,2,64,128]{3,2,1,0:T(8,128)(2,1)S(1)} %get-tuple-element.48), channel_id=1, source_target_pairs={{1,2},{2,1},{3,4},{4,3},{5,6},{6,5},{7,8},{8,7},{9,10},{10,9},{11,... | collective-permute-start | bytes 294920 | tf_op jit(solution)/shard_map/ppermute | solution.py:260
  28.6 0.1 collective-permute-start.6
  28.7 2.8 %collective-permute-start.7 = (bf16[2,64,128]{2,1,0:T(8,128)(2,1)S(1)}, bf16[2,64,128]{2,1,0:T(8,128)(2,1)S(1)}, u32[]{:S(2)}, u32[]{:S(2)}) collective-permute-start(bf16[2,64,128]{2,1,0:T(8,128)(2,1)S(1)} %get-tuple-element.50), channel_id=1, source_target_pairs={{64,128},{128,64},{65,129},{129,65},{66,130},{130,66},{67,131},{13... | collective-permute-start | bytes 98312 | tf_op jit(solution)/shard_map/ppermute | solution.py:260
  31.6 0.0 collective-permute-done.6.slab_a
  31.6 1.8 %collective-permute-done.7.slab_b = bf16[2,64,128]{2,1,0:T(8,128)(2,1)S(1)} collective-permute-done((bf16[2,64,128]{2,1,0:T(8,128)(2,1)S(1)}, bf16[2,64,128]{2,1,0:T(8,128)(2,1)S(1)}, u32[]{:S(2)}, u32[]{:S(2)}) %collective-permute-start.7) | collective-permute-done | bytes 32800 | tf_op jit(solution)/shard_map/ppermute | solution.py:260
  33.4 0.0 collective-permute-done.4.core
  33.4 0.0 collective-permute-done.5.rng
  33.4 3.7 %conv1.1 = (bf16[2,512,128]{2,1,0:T(8,128)(2,1)S(1)}, bf16[3,2,64,128]{3,2,1,0:T(8,128)(2,1)S(1)}, bf16[3,2,64,128]{3,2,1,0:T(8,128)(2,1)S(1)}, bf16[3,2,64,128]...) custom-call(s32[2]{0:T(128)S(1)} %copy-done.10, ...), custom_call_target="tpu_custom_call" | custom-call | tf_op jit(solution)/shard_map/conv1/pallas_call | solution.py:315
  37.2 0.1 collective-permute-start.8
  37.3 3.9 %collective-permute-start.9 = (bf16[3,2,64,128]{3,2,1,0:T(8,128)(2,1)S(1)}, bf16[3,2,64,128]{3,2,1,0:T(8,128)(2,1)S(1)}, u32[]{:S(2)}, u32[]{:S(2)}) collective-permute-start(bf16[3,2,64,128]{3,2,1,0:T(8,128)(2,1)S(1)} %get-tuple-element.55), channel_id=1, source_target_pairs={{1,2},{2,1},{3,4},{4,3},{5,6},{6,5},{7,8},{8,7},{9,10},{10,9},{11,... | collective-permute-start | bytes 294920 | tf_op jit(solution)/shard_map/ppermute | solution.py:260
  41.2 0.1 collective-permute-start.10
  41.3 2.5 %collective-permute-start.11 = (bf16[2,64,128]{2,1,0:T(8,128)(2,1)S(1)}, bf16[2,64,128]{2,1,0:T(8,128)(2,1)S(1)}, u32[]{:S(2)}, u32[]{:S(2)}) collective-permute-start(bf16[2,64,128]{2,1,0:T(8,128)(2,1)S(1)} %get-tuple-element.57), channel_id=1, source_target_pairs={{64,128},{128,64},{65,129},{129,65},{66,130},{130,66},{67,131},{13... | collective-permute-start | bytes 98312 | tf_op jit(solution)/shard_map/ppermute | solution.py:260
  43.8 0.3 collective-permute-done.10.slab_a
  44.0 1.9 %collective-permute-done.11.slab_b = bf16[2,64,128]{2,1,0:T(8,128)(2,1)S(1)} collective-permute-done((bf16[2,64,128]{2,1,0:T(8,128)(2,1)S(1)}, bf16[2,64,128]{2,1,0:T(8,128)(2,1)S(1)}, u32[]{:S(2)}, u32[]{:S(2)}) %collective-permute-start.11) | collective-permute-done | bytes 32800 | tf_op jit(solution)/shard_map/ppermute | solution.py:260
  45.9 0.0 collective-permute-done.8.core
  45.9 0.0 collective-permute-done.9.rng
  46.0 3.7 %conv2.1 = (bf16[2,512,128]{2,1,0:T(8,128)(2,1)S(1)}, bf16[3,2,64,128]{3,2,1,0:T(8,128)(2,1)S(1)}, bf16[3,2,64,128]{3,2,1,0:T(8,128)(2,1)S(1)}, bf16[3,2,64,128]...) custom-call(s32[2]{0:T(128)S(1)} %copy-done.10, ...), custom_call_target="tpu_custom_call" | custom-call | tf_op jit(solution)/shard_map/conv2/pallas_call | solution.py:315
  49.7 0.1 collective-permute-start.12
  49.8 5.1 %collective-permute-start.13 = (bf16[3,2,64,128]{3,2,1,0:T(8,128)(2,1)S(1)}, bf16[3,2,64,128]{3,2,1,0:T(8,128)(2,1)S(1)}, u32[]{:S(2)}, u32[]{:S(2)}) collective-permute-start(bf16[3,2,64,128]{3,2,1,0:T(8,128)(2,1)S(1)} %get-tuple-element.62), channel_id=1, source_target_pairs={{1,2},{2,1},{3,4},{4,3},{5,6},{6,5},{7,8},{8,7},{9,10},{10,9},{11,... | collective-permute-start | bytes 294920 | tf_op jit(solution)/shard_map/ppermute | solution.py:260
  54.9 0.1 collective-permute-start.14
  55.0 1.9 %collective-permute-start.15 = (bf16[2,64,128]{2,1,0:T(8,128)(2,1)S(1)}, bf16[2,64,128]{2,1,0:T(8,128)(2,1)S(1)}, u32[]{:S(2)}, u32[]{:S(2)}) collective-permute-start(bf16[2,64,128]{2,1,0:T(8,128)(2,1)S(1)} %get-tuple-element.64), channel_id=1, source_target_pairs={{64,128},{128,64},{65,129},{129,65},{66,130},{130,66},{67,131},{13... | collective-permute-start | bytes 98312 | tf_op jit(solution)/shard_map/ppermute | solution.py:260
  56.9 0.8 collective-permute-done.14.slab_a
  57.8 1.9 %collective-permute-done.15.slab_b = bf16[2,64,128]{2,1,0:T(8,128)(2,1)S(1)} collective-permute-done((bf16[2,64,128]{2,1,0:T(8,128)(2,1)S(1)}, bf16[2,64,128]{2,1,0:T(8,128)(2,1)S(1)}, u32[]{:S(2)}, u32[]{:S(2)}) %collective-permute-start.15) | collective-permute-done | bytes 32800 | tf_op jit(solution)/shard_map/ppermute | solution.py:260
  59.7 0.0 collective-permute-done.12.core
  59.7 0.0 collective-permute-done.13.rng
  59.7 3.9 %conv3.1 = bf16[128,64,128]{2,1,0:T(8,128)(2,1)S(1)} custom-call(s32[2]{0:T(128)S(1)} %copy-done.10, s32[2,26]{1,0:T(2,128)S(1)} %copy-done.9, bf16[2,512,128]{2,1,0:T(8,128)(2,1)S(1)} %get-tuple-element.58.act, bf16[3,2,64,128]{3,2,1,0:T(8,128)(2,1)S(1)} %get-tuple-element.59.last, bf16[3,2,64,128]{3,2,1,0:T(8,128)(2,1)S(1)} %get-tuple-element.60.first, ...), custom_call_target="tpu_custom_call" | custom-call | tf_op jit(solution)/shard_map/conv3/pallas_call | solution.py:315
  63.5 63.1 %all_to_all.5.octants = bf16[128,64,128]{2,1,0:T(8,128)(2,1)} all-to-all(bf16[128,64,128]{2,1,0:T(8,128)(2,1)S(1)} %conv3.1), channel_id=1, replica_groups=mesh['slab'=4,'range'=64] {'range'}, dimensions={0} | all-to-all | bytes 4194304 | tf_op jit(solution)/shard_map/all_to_all | solution.py:336
  126.6 12.4 %grow.1 = bf16[128,64,512]{2,1,0:T(8,128)(2,1)} custom-call(bf16[128,64,128]{2,1,0:T(8,128)(2,1)} %all_to_all.5.octants, bf16[128,512]{1,0:T(8,128)(2,1)} %up.1), custom_call_target="tpu_custom_call" | custom-call | tf_op jit(solution)/shard_map/grow/pallas_call | solution.py:338
  (16 shorter events, 0.0 us)
Async XLA Ops:
  0.0 33.4 %copy-start.2 = (bf16[2,512,128]{2,1,0:T(8,128)(2,1)S(1)}, bf16[2,512,128]{2,1,0:T(8,128)(2,1)}, u32[]{:S(2)}) copy-start(bf16[2,512,128]{2,1,0:T(8,128)(2,1)} %rest_0_.1) | copy-start | bytes 786436
  3.4 30.0 %copy-start.9 = (s32[2,26]{1,0:T(2,128)S(1)}, s32[2,26]{1,0:T(2,128)}, u32[]{:S(2)}) copy-start(s32[2,26]{1,0:T(2,128)} %get-tuple-element.36.faces) | copy-start | bytes 628
  3.5 10.1 %collective-permute-start = (bf16[3,2,64,128]{3,2,1,0:T(8,128)(2,1)}, bf16[3,2,64,128]{3,2,1,0:T(8,128)(2,1)S(1)}, u32[]{:S(2)}, u32[]{:S(2)}) collective-permute-start(bf16[3,2,64,128]{3,2,1,0:T(8,128)(2,1)} %get-tuple-element.40), channel_id=1, source_target_pairs={{0,1},{1,0},{2,3},{3,2},{4,5},{5,4},{6,7},{7,6},{8,9},{9,8},{10,11... | collective-permute-start | bytes 294920 | tf_op jit(solution)/shard_map/ppermute | solution.py:260
  4.2 9.3 %collective-permute-start.1 = (bf16[3,2,64,128]{3,2,1,0:T(8,128)(2,1)}, bf16[3,2,64,128]{3,2,1,0:T(8,128)(2,1)S(1)}, u32[]{:S(2)}, u32[]{:S(2)}) collective-permute-start(bf16[3,2,64,128]{3,2,1,0:T(8,128)(2,1)} %get-tuple-element.41), channel_id=1, source_target_pairs={{1,2},{2,1},{3,4},{4,3},{5,6},{6,5},{7,8},{8,7},{9,10},{10,9},{11,... | collective-permute-start | bytes 294920 | tf_op jit(solution)/shard_map/ppermute | solution.py:260
  7.7 3.1 %collective-permute-start.2 = (bf16[2,64,128]{2,1,0:T(8,128)(2,1)}, bf16[2,64,128]{2,1,0:T(8,128)(2,1)S(1)}, u32[]{:S(2)}, u32[]{:S(2)}) collective-permute-start(bf16[2,64,128]{2,1,0:T(8,128)(2,1)} %get-tuple-element.42), channel_id=1, source_target_pairs={{0,64},{64,0},{128,192},{192,128},{1,65},{65,1},{129,193},{193,129... | collective-permute-start | bytes 98312 | tf_op jit(solution)/shard_map/ppermute | solution.py:260
  8.7 4.9 %collective-permute-start.3 = (bf16[2,64,128]{2,1,0:T(8,128)(2,1)}, bf16[2,64,128]{2,1,0:T(8,128)(2,1)S(1)}, u32[]{:S(2)}, u32[]{:S(2)}) collective-permute-start(bf16[2,64,128]{2,1,0:T(8,128)(2,1)} %get-tuple-element.43), channel_id=1, source_target_pairs={{64,128},{128,64},{65,129},{129,65},{66,130},{130,66},{67,131},{13... | collective-permute-start | bytes 98312 | tf_op jit(solution)/shard_map/ppermute | solution.py:260
  13.5 2.0 %copy-start = (bf16[4,27,128,128]{3,2,1,0:T(8,128)(2,1)S(1)}, bf16[4,27,128,128]{3,2,1,0:T(8,128)(2,1)}, u32[]{:S(2)}) copy-start(bf16[4,27,128,128]{3,2,1,0:T(8,128)(2,1)} %param.14) | copy-start | bytes 10616836
  15.5 0.9 copy-start.3
  16.5 0.9 copy-start.4
  17.4 0.9 copy-start.5
  18.3 0.7 copy-start.6
  19.0 0.7 copy-start.7
  19.6 0.7 copy-start.8
  20.3 0.6 copy-start.10
  20.9 12.5 %copy-start.1 = (bf16[4,27,128,128]{3,2,1,0:T(8,128)(2,1)S(1)}, bf16[4,27,128,128]{3,2,1,0:T(8,128)(2,1)}, u32[]{:S(2)}) copy-start(bf16[4,27,128,128]{3,2,1,0:T(8,128)(2,1)} %param.14) | copy-start | bytes 10616836
  24.6 8.8 %collective-permute-start.4 = (bf16[3,2,64,128]{3,2,1,0:T(8,128)(2,1)S(1)}, bf16[3,2,64,128]{3,2,1,0:T(8,128)(2,1)S(1)}, u32[]{:S(2)}, u32[]{:S(2)}) collective-permute-start(bf16[3,2,64,128]{3,2,1,0:T(8,128)(2,1)S(1)} %get-tuple-element.47), channel_id=1, source_target_pairs={{0,1},{1,0},{2,3},{3,2},{4,5},{5,4},{6,7},{7,6},{8,9},{9,8},{10,11... | collective-permute-start | bytes 294920 | tf_op jit(solution)/shard_map/ppermute | solution.py:260
  24.7 8.7 %collective-permute-start.5 = (bf16[3,2,64,128]{3,2,1,0:T(8,128)(2,1)S(1)}, bf16[3,2,64,128]{3,2,1,0:T(8,128)(2,1)S(1)}, u32[]{:S(2)}, u32[]{:S(2)}) collective-permute-start(bf16[3,2,64,128]{3,2,1,0:T(8,128)(2,1)S(1)} %get-tuple-element.48), channel_id=1, source_target_pairs={{1,2},{2,1},{3,4},{4,3},{5,6},{6,5},{7,8},{8,7},{9,10},{10,9},{11,... | collective-permute-start | bytes 294920 | tf_op jit(solution)/shard_map/ppermute | solution.py:260
  28.6 2.9 %collective-permute-start.6 = (bf16[2,64,128]{2,1,0:T(8,128)(2,1)S(1)}, bf16[2,64,128]{2,1,0:T(8,128)(2,1)S(1)}, u32[]{:S(2)}, u32[]{:S(2)}) collective-permute-start(bf16[2,64,128]{2,1,0:T(8,128)(2,1)S(1)} %get-tuple-element.49), channel_id=1, source_target_pairs={{0,64},{64,0},{128,192},{192,128},{1,65},{65,1},{129,193},{193,129... | collective-permute-start | bytes 98312 | tf_op jit(solution)/shard_map/ppermute | solution.py:260
  28.7 4.7 %collective-permute-start.7 = (bf16[2,64,128]{2,1,0:T(8,128)(2,1)S(1)}, bf16[2,64,128]{2,1,0:T(8,128)(2,1)S(1)}, u32[]{:S(2)}, u32[]{:S(2)}) collective-permute-start(bf16[2,64,128]{2,1,0:T(8,128)(2,1)S(1)} %get-tuple-element.50), channel_id=1, source_target_pairs={{64,128},{128,64},{65,129},{129,65},{66,130},{130,66},{67,131},{13... | collective-permute-start | bytes 98312 | tf_op jit(solution)/shard_map/ppermute | solution.py:260
  33.4 26.2 %copy-start.11 = (s32[16]{0:T(128)S(1)}, s32[16]{0:T(128)}, u32[]{:S(2)}) copy-start(s32[16]{0:T(128)} %get-tuple-element.66.rest_1_) | copy-start | bytes 196
  37.2 8.8 %collective-permute-start.8 = (bf16[3,2,64,128]{3,2,1,0:T(8,128)(2,1)S(1)}, bf16[3,2,64,128]{3,2,1,0:T(8,128)(2,1)S(1)}, u32[]{:S(2)}, u32[]{:S(2)}) collective-permute-start(bf16[3,2,64,128]{3,2,1,0:T(8,128)(2,1)S(1)} %get-tuple-element.54), channel_id=1, source_target_pairs={{0,1},{1,0},{2,3},{3,2},{4,5},{5,4},{6,7},{7,6},{8,9},{9,8},{10,11... | collective-permute-start | bytes 294920 | tf_op jit(solution)/shard_map/ppermute | solution.py:260
  37.3 8.7 %collective-permute-start.9 = (bf16[3,2,64,128]{3,2,1,0:T(8,128)(2,1)S(1)}, bf16[3,2,64,128]{3,2,1,0:T(8,128)(2,1)S(1)}, u32[]{:S(2)}, u32[]{:S(2)}) collective-permute-start(bf16[3,2,64,128]{3,2,1,0:T(8,128)(2,1)S(1)} %get-tuple-element.55), channel_id=1, source_target_pairs={{1,2},{2,1},{3,4},{4,3},{5,6},{6,5},{7,8},{8,7},{9,10},{10,9},{11,... | collective-permute-start | bytes 294920 | tf_op jit(solution)/shard_map/ppermute | solution.py:260
  41.2 2.9 %collective-permute-start.10 = (bf16[2,64,128]{2,1,0:T(8,128)(2,1)S(1)}, bf16[2,64,128]{2,1,0:T(8,128)(2,1)S(1)}, u32[]{:S(2)}, u32[]{:S(2)}) collective-permute-start(bf16[2,64,128]{2,1,0:T(8,128)(2,1)S(1)} %get-tuple-element.56), channel_id=1, source_target_pairs={{0,64},{64,0},{128,192},{192,128},{1,65},{65,1},{129,193},{193,129... | collective-permute-start | bytes 98312 | tf_op jit(solution)/shard_map/ppermute | solution.py:260
  41.3 4.7 %collective-permute-start.11 = (bf16[2,64,128]{2,1,0:T(8,128)(2,1)S(1)}, bf16[2,64,128]{2,1,0:T(8,128)(2,1)S(1)}, u32[]{:S(2)}, u32[]{:S(2)}) collective-permute-start(bf16[2,64,128]{2,1,0:T(8,128)(2,1)S(1)} %get-tuple-element.57), channel_id=1, source_target_pairs={{64,128},{128,64},{65,129},{129,65},{66,130},{130,66},{67,131},{13... | collective-permute-start | bytes 98312 | tf_op jit(solution)/shard_map/ppermute | solution.py:260
  49.7 10.0 %collective-permute-start.12 = (bf16[3,2,64,128]{3,2,1,0:T(8,128)(2,1)S(1)}, bf16[3,2,64,128]{3,2,1,0:T(8,128)(2,1)S(1)}, u32[]{:S(2)}, u32[]{:S(2)}) collective-permute-start(bf16[3,2,64,128]{3,2,1,0:T(8,128)(2,1)S(1)} %get-tuple-element.61), channel_id=1, source_target_pairs={{0,1},{1,0},{2,3},{3,2},{4,5},{5,4},{6,7},{7,6},{8,9},{9,8},{10,11... | collective-permute-start | bytes 294920 | tf_op jit(solution)/shard_map/ppermute | solution.py:260
  49.8 9.9 %collective-permute-start.13 = (bf16[3,2,64,128]{3,2,1,0:T(8,128)(2,1)S(1)}, bf16[3,2,64,128]{3,2,1,0:T(8,128)(2,1)S(1)}, u32[]{:S(2)}, u32[]{:S(2)}) collective-permute-start(bf16[3,2,64,128]{3,2,1,0:T(8,128)(2,1)S(1)} %get-tuple-element.62), channel_id=1, source_target_pairs={{1,2},{2,1},{3,4},{4,3},{5,6},{6,5},{7,8},{8,7},{9,10},{10,9},{11,... | collective-permute-start | bytes 294920 | tf_op jit(solution)/shard_map/ppermute | solution.py:260
  54.9 2.9 %collective-permute-start.14 = (bf16[2,64,128]{2,1,0:T(8,128)(2,1)S(1)}, bf16[2,64,128]{2,1,0:T(8,128)(2,1)S(1)}, u32[]{:S(2)}, u32[]{:S(2)}) collective-permute-start(bf16[2,64,128]{2,1,0:T(8,128)(2,1)S(1)} %get-tuple-element.63), channel_id=1, source_target_pairs={{0,64},{64,0},{128,192},{192,128},{1,65},{65,1},{129,193},{193,129... | collective-permute-start | bytes 98312 | tf_op jit(solution)/shard_map/ppermute | solution.py:260
  55.0 4.7 %collective-permute-start.15 = (bf16[2,64,128]{2,1,0:T(8,128)(2,1)S(1)}, bf16[2,64,128]{2,1,0:T(8,128)(2,1)S(1)}, u32[]{:S(2)}, u32[]{:S(2)}) collective-permute-start(bf16[2,64,128]{2,1,0:T(8,128)(2,1)S(1)} %get-tuple-element.64), channel_id=1, source_target_pairs={{64,128},{128,64},{65,129},{129,65},{66,130},{130,66},{67,131},{13... | collective-permute-start | bytes 98312 | tf_op jit(solution)/shard_map/ppermute | solution.py:260
where the time goes:
time: 140 us; the launch traced here: 139 us
  blocking collectives  63.1 us (45%)
  Pallas kernels  30.3 us (22%)
  starting transfers between devices  27.9 us (20%)
  waiting for transfers between devices  9.69 us (7%)
  local copies, waits for them, and re-layouts  7.35 us (5%)
    all_to_all x1, blocking collectives, shards(): lax.all_to_all(result[0], 'range', split_axis=0, concat_axis=0, tiled=True)  63.1 us
    ppermute x16, starting transfers between devices, swap(): return lax.ppermute(block, axis, route)  27.9 us
    pallas_call x4, Pallas kernels, shards(): pl.pallas_call(functools.partial(conv_kernel, step), out_shape=outs, in_s...  15 us
    pallas_call x1, Pallas kernels, shards(): pl.pallas_call(grow_kernel, grid=(128 // slab,), out_shape=bf16(128, OCT,...  12.4 us
    ppermute x16, waiting for transfers between devices, swap(): return lax.ppermute(block, axis, route)  9.69 us
    unnamed x24, local copies, waits for them, and re-layouts  7.35 us
    pallas_call x1, Pallas kernels, shards(): pl.pallas_call(start_kernel, out_shape=[bf16(BRICKS, VOX, CH), *SENDS, ja...  2.88 us
  transfers between devices with their start and end apart: 16, of which 7 were waited for; matrix products, arithmetic and copies ran while one was open for 0% of the time, Pallas kernels for 0%

commit v1 on v0

--- a/solution.py
+++ b/solution.py
@@ -27,6 +27,7 @@
 VMEM = pl.BlockSpec(memory_space=pltpu.VMEM)
 SMEM = pl.BlockSpec(memory_space=pltpu.SMEM)
 ANY = pl.BlockSpec(memory_space=pl.ANY)
+HBM = pl.BlockSpec(memory_space=pltpu.HBM)
 
 
 def group_sum(rows):
@@ -47,7 +48,7 @@
     return w * (0.5 + 0.5 * jnp.tanh(0.5 * w))
 
 
-def emit_active(load, b, gain, shift, info, act_s, act, sends):
+def emit_active(load, b, gain, shift, act_s, act, sends):
     value = normalize(load, gain, shift)
     act_s[pl.ds(b * VOX, VOX)] = value.reshape(VOX, CH)
     act[b] = value.reshape(VOX, CH).astype(jnp.bfloat16)
@@ -61,7 +62,11 @@
             plane[2, b, rows] = act_s[pl.ds(base + x * 64 + side, 8, stride=8)].astype(jnp.bfloat16)
 
 
-def choose_sends(info, sends):
+def parity(axis):
+    return lax.rem(lax.axis_index(axis), 2)
+
+
+def choose_sends(sends):
     last, first, to_core, to_range, to_a, to_b = sends
 
     def route(flag, yes, no):
@@ -75,20 +80,36 @@
             yes[...] = first[...] if yes.shape[0] == 3 else first[0]
             no[...] = last[...] if no.shape[0] == 3 else last[0]
 
-    route(info[0], to_core, to_range)
-    route(info[1], to_a, to_b)
+    route(parity("range"), to_core, to_range)
+    route(parity("slab"), to_a, to_b)
+
+
+def fetch(sems, *pairs):
+    copies = [pltpu.make_async_copy(src, dst, sems.at[i]) for i, (src, dst) in enumerate(pairs)]
+    for copy in copies:
+        copy.start()
+    return copies
 
 
 def start_kernel(
-    info, features, neighbours, kept, owner, gain, shift,
-    act, last, first, to_core, to_range, to_a, to_b, faces, slots, act_s,
+    features_hbm, gain_hbm, shift_hbm, act, last, first, to_core, to_range, to_a, to_b,
+    act_s, features, gain, shift, sems,
 ):
+    copies = fetch(sems, (gain_hbm, gain), (shift_hbm, shift), *[(features_hbm.at[b], features.at[b]) for b in range(BRICKS)])
+    for copy in copies[:2]:
+        copy.wait()
     sends = (last, first, to_core, to_range, to_a, to_b)
     for b in range(BRICKS):
+        copies[2 + b].wait()
         load = lambda b=b: features[b].astype(jnp.float32).reshape(OCT, EDGE, CH)
-        emit_active(load, b, gain[0:1], shift[0:1], info, act_s, act, sends)
-    choose_sends(info, sends)
-    odd_range, odd_slab = info[0], info[1]
+        emit_active(load, b, gain[0:1], shift[0:1], act_s, act, sends)
+    choose_sends(sends)
+
+
+def route_kernel(neighbours_hbm, kept_hbm, owner_hbm, after, faces, slots, neighbours, kept, owner, sems):
+    for copy in fetch(sems, (neighbours_hbm, neighbours), (kept_hbm, kept), (owner_hbm, owner)):
+        copy.wait()
+    odd_range, odd_slab = parity("range"), parity("slab")
     below = jnp.where(odd_range == 1, CORE, RANGE)
     above = jnp.where(odd_range == 1, RANGE, CORE)
     under = jnp.where(odd_slab == 1, SLAB_A, SLAB_B)
@@ -187,7 +208,7 @@
 
 
 def conv_kernel(
-    step, info, faces, act, last, first, core, rng, slab_a, slab_b, weights_hbm, gain, shift, *rest,
+    step, faces, act, last, first, core, rng, slab_a, slab_b, weights_hbm, gain_hbm, shift_hbm, *rest,
 ):
     rest = list(rest)
     state = rest.pop(0) if step % 2 else None
@@ -198,13 +219,16 @@
         act_out = rest.pop(0)
         sends = [rest.pop(0) for _ in range(6)]
         state_out = rest.pop(0) if step == 1 else None
-    table, field, window, weights, total, act_s, sem = rest
-    copy = pltpu.make_async_copy(weights_hbm.at[step], weights, sem)
-    copy.start()
+    table, field, window, weights, total, act_s, gain, shift, sems = rest
+    pairs = [(weights_hbm.at[step], weights)]
+    if step < 3:
+        pairs += [(gain_hbm, gain), (shift_hbm, shift)]
+    copies = fetch(sems, *pairs)
     assemble(act, faces, (last, first, core, rng, slab_a, slab_b), table, field, window)
     if step == 3:
         packed[...] = jnp.zeros(packed.shape, packed.dtype)
-    copy.wait()
+    for copy in copies:
+        copy.wait()
     convolve(window, weights, total)
     for b in range(BRICKS):
         if step % 2:
@@ -217,9 +241,9 @@
             total[:, b] = total[:, b].astype(jnp.bfloat16).astype(jnp.float32)
         if step < 3:
             load = lambda b=b: total[:, b]
-            emit_active(load, b, gain[step + 1 : step + 2], shift[step + 1 : step + 2], info, act_s, act_out, sends)
+            emit_active(load, b, gain[step + 1 : step + 2], shift[step + 1 : step + 2], act_s, act_out, sends)
     if step < 3:
-        choose_sends(info, sends)
+        choose_sends(sends)
         return
     low = lax.broadcasted_iota(jnp.int32, (4, 2, 8, CH), 2) < 4
     for b in range(BRICKS):
@@ -255,8 +279,7 @@
     route = []
     for i in range(count):
         j = (i ^ 1) if not odd else (i + 1 if i % 2 else i - 1)
-        if 0 <= j < count:
-            route.append((i, j))
+        route.append((i, j % count))
     return lax.ppermute(block, axis, route)
 
 
@@ -280,27 +303,50 @@
     bf16(BRICKS, FACE, CH),
     bf16(BRICKS, FACE, CH),
 ]
-LIMIT = 48 * 1024 * 1024
+LIMIT = 16 * 1024 * 1024
 
 
 def shards(features, neighbours, keep_mask, owner, norm_gain, norm_shift, conv_weights, up_weight):
-    info = jnp.stack([lax.axis_index("range") % 2, lax.axis_index("slab") % 2]).astype(jnp.int32)
     act_s = pltpu.VMEM((BRICKS * VOX, CH), jnp.float32)
-    act, *sends, faces, slots = pl.pallas_call(
+    norm_s = [pltpu.VMEM((4, CH), jnp.float32)] * 2
+    in_hbm = lambda v: pltpu.with_memory_space_constraint(v, pltpu.HBM)
+    gain, shift = in_hbm(norm_gain), in_hbm(norm_shift)
+    act, *sends = pl.pallas_call(
         start_kernel,
-        out_shape=[bf16(BRICKS, VOX, CH), *SENDS, jax.ShapeDtypeStruct((BRICKS, 26), jnp.int32),
-                   jax.ShapeDtypeStruct((8 * BRICKS,), jnp.int32)],
-        in_specs=[SMEM, VMEM, SMEM, SMEM, SMEM, VMEM, VMEM],
-        out_specs=[VMEM] * 7 + [SMEM, SMEM],
-        scratch_shapes=[act_s],
+        out_shape=[bf16(BRICKS, VOX, CH), *SENDS],
+        in_specs=[HBM] * 3,
+        out_specs=[VMEM] * 7,
+        scratch_shapes=[
+            act_s,
+            pltpu.VMEM((BRICKS, VOX, CH), jnp.bfloat16),
+            *norm_s,
+            pltpu.SemaphoreType.DMA((2 + BRICKS,)),
+        ],
+        compiler_params=pltpu.CompilerParams(vmem_limit_bytes=LIMIT),
+        cost_estimate=pl.CostEstimate(flops=10**7, bytes_accessed=2**22, transcendentals=2**17),
         name="start",
-    )(info, features, neighbours, keep_mask, owner, norm_gain, norm_shift)
-    weights = conv_weights.reshape(4, 27 * CH, CH)
+    )(in_hbm(features), gain, shift)
+    faces, slots = pl.pallas_call(
+        route_kernel,
+        out_shape=[jax.ShapeDtypeStruct((BRICKS, 26), jnp.int32), jax.ShapeDtypeStruct((8 * BRICKS,), jnp.int32)],
+        in_specs=[HBM, HBM, HBM, ANY],
+        out_specs=[SMEM, SMEM],
+        scratch_shapes=[
+            pltpu.SMEM((BRICKS, 26), jnp.int32),
+            pltpu.SMEM((BRICKS, 8), jnp.int32),
+            pltpu.SMEM((BRICKS, 8), jnp.int32),
+            pltpu.SemaphoreType.DMA((3,)),
+        ],
+        compiler_params=pltpu.CompilerParams(vmem_limit_bytes=LIMIT),
+        cost_estimate=pl.CostEstimate(flops=1000, bytes_accessed=4096, transcendentals=0),
+        name="route",
+    )(in_hbm(neighbours), in_hbm(keep_mask), in_hbm(owner), act)
+    weights = in_hbm(conv_weights.reshape(4, 27 * CH, CH))
     state = features
     for step in range(4):
         planes = exchange(sends)
-        inputs = [info, faces, act, *planes, weights, norm_gain, norm_shift]
-        in_specs = [SMEM, SMEM] + [VMEM] * 7 + [ANY, VMEM, VMEM]
+        inputs = [faces, act, *planes, weights, gain, shift]
+        in_specs = [SMEM] + [VMEM] * 7 + [HBM] * 3
         if step % 2:
             inputs.append(state)
             in_specs.append(VMEM)
@@ -324,9 +370,11 @@
                 pltpu.VMEM((27 * CH, CH), jnp.bfloat16),
                 pltpu.VMEM((OCT, BRICKS, EDGE, CH), jnp.float32),
                 act_s,
-                pltpu.SemaphoreType.DMA,
+                *norm_s,
+                pltpu.SemaphoreType.DMA((3,)),
             ],
             compiler_params=pltpu.CompilerParams(vmem_limit_bytes=LIMIT),
+            cost_estimate=pl.CostEstimate(flops=2 * 10**9, bytes_accessed=2**22, transcendentals=2**17),
             name=f"conv{step}",
         )(*inputs)
         if step < 3:
@@ -334,7 +382,7 @@
             if step == 1:
                 state = result[7]
     arrived = lax.all_to_all(result[0], "range", split_axis=0, concat_axis=0, tiled=True)
-    slab = 8
+    slab = 32
     return pl.pallas_call(
         grow_kernel,
         grid=(128 // slab,),
@@ -344,6 +392,7 @@
             pl.BlockSpec((CH, 4 * CH), lambda i: (0, 0)),
         ],
         out_specs=pl.BlockSpec((slab, OCT, 4 * CH), lambda i: (i, 0, 0)),
+        compiler_params=pltpu.CompilerParams(vmem_limit_bytes=32 * 1024 * 1024),
         name="grow",
     )(arrived, up_weight)
 

time: 140 us -> 118 us (0.84)
  local copies, waits for them, and re-layouts: 7.35 us -> 0.01 us
  blocking collectives: 63.1 us -> 58.1 us
  Pallas kernels: 30.3 us -> 25.7 us
  starting transfers between devices: 27.9 us -> 23.7 us
  waiting for transfers between devices: 9.69 us -> 8.24 us
    pallas_call x1, Pallas kernels: 12.4 us -> 4.7 us  [shards(): pl.pallas_call(grow_kernel, grid=(128 // slab,), out_shape=bf16(128, OCT,...]
    unnamed x24 -> x4, local copies, waits for them, and re-layouts: 7.35 us -> 0.01 us
    all_to_all x1, blocking collectives: 63.1 us -> 58.1 us  [shards(): lax.all_to_all(result[0], 'range', split_axis=0, concat_axis=0, tiled=True)]
    ppermute x16, starting transfers between devices: 27.9 us -> 23.7 us  [swap(): return lax.ppermute(block, axis, route)]
    pallas_call x4, Pallas kernels: 15 us -> 16.9 us  [shards(): pl.pallas_call(functools.partial(conv_kernel, step), out_shape=outs, in_s...]
    ppermute x16, waiting for transfers between devices: 9.69 us -> 8.24 us  [swap(): return lax.ppermute(block, axis, route)]
    pallas_call x1 -> x2, Pallas kernels: 2.88 us -> 4.14 us  [the longest x1 2.08 us: shards(): pl.pallas_call(start_kernel, out_shape=[bf16(BRICKS, VOX, CH), *SENDS], i...]
  transfers between devices with their start and end apart: 16 -> 16, of which waited for: 7 -> 7; matrix products, arithmetic and copies ran while one was open for 0% -> 0% of each run, Pallas kernels for 0% -> 2%
where the time goes in v1:
time: 118 us; the launch traced here: 116 us
  blocking collectives  58.1 us (49%)
  Pallas kernels  25.7 us (22%)
  starting transfers between devices  23.7 us (20%)
  waiting for transfers between devices  8.24 us (7%)
    all_to_all x1, blocking collectives, shards(): lax.all_to_all(result[0], 'range', split_axis=0, concat_axis=0, tiled=True)  58.1 us
    ppermute x16, starting transfers between devices, swap(): return lax.ppermute(block, axis, route)  23.7 us
    pallas_call x4, Pallas kernels, shards(): pl.pallas_call(functools.partial(conv_kernel, step), out_shape=outs, in_s...  16.9 us
    ppermute x16, waiting for transfers between devices, swap(): return lax.ppermute(block, axis, route)  8.24 us
    pallas_call x1, Pallas kernels, shards(): pl.pallas_call(grow_kernel, grid=(128 // slab,), out_shape=bf16(128, OCT,...  4.7 us
  transfers between devices with their start and end apart: 16, of which 7 were waited for; matrix products, arithmetic and copies ran while one was open for 0% of the time, Pallas kernels for 2%

profile of v1, /device:TPU:5, one launch (start us, length us, event | category | flops | bytes accessed | tf_op | source)
XLA Modules:
  0.0 115.9 jit_solution(9901661131017776519)
XLA Ops:
  0.0 2.1 %start.1 = (bf16[2,512,128]{2,1,0:T(8,128)(2,1)S(1)}, bf16[3,2,64,128]{3,2,1,0:T(8,128)(2,1)S(1)}, bf16[3,2,64,128]{3,2,1,0:T(8,128)(2,1)S(1)}, bf16[3,2,64,128]...) custom-call(bf16[2,512,128]{2,1,0:T(8,128)(2,1)} %rest_0_.1, ...), custom_call_target="tpu_custom_call" | custom-call | flops 10000000 | bytes 4194304 | tf_op jit(solution)/shard_map/start/pallas_call | solution.py:314
  2.1 0.8 collective-permute-start
  2.9 1.6 %collective-permute-start.1 = (bf16[3,2,64,128]{3,2,1,0:T(8,128)(2,1)S(1)}, bf16[3,2,64,128]{3,2,1,0:T(8,128)(2,1)S(1)}, u32[]{:S(2)}, u32[]{:S(2)}) collective-permute-start(bf16[3,2,64,128]{3,2,1,0:T(8,128)(2,1)S(1)} %get-tuple-element.41), channel_id=1, source_target_pairs={{0,63},{1,2},{2,1},{3,4},{4,3},{5,6},{6,5},{7,8},{8,7},{9,10},{10,... | collective-permute-start | bytes 294920 | tf_op jit(solution)/shard_map/ppermute | solution.py:283
  4.5 0.9 collective-permute-start.2
  5.4 0.0 collective-permute-start.3
  5.4 2.1 %route.1 = (s32[2,26]{1,0:T(2,128)S(1)}, s32[16]{0:T(128)S(1)}) custom-call(s32[2,26]{1,0:T(2,128)} %neighbours_hbm.1, s32[2,8]{1,0:T(2,128)} %kept_hbm.1, s32[2,8]{1,0:T(2,128)} %owner_hbm.1, bf16[2,512,128]{2,1,0:T(8,128)(2,1)S(1)} %get-tuple-element.36.after.act), custom_call_target="tpu_custom_call" | custom-call | flops 1000 | bytes 4096 | tf_op jit(solution)/shard_map/route/pallas_call | solution.py:329
  7.5 0.0 collective-permute-done.2.slab_a
  7.5 0.7 collective-permute-done.3.slab_b
  8.2 0.0 collective-permute-done.core
  8.2 0.0 collective-permute-done.1.rng
  8.2 0.0 copy-start
  8.2 4.3 %conv0.1 = (bf16[2,512,128]{2,1,0:T(8,128)(2,1)S(1)}, bf16[3,2,64,128]{3,2,1,0:T(8,128)(2,1)S(1)}, bf16[3,2,64,128]{3,2,1,0:T(8,128)(2,1)S(1)}, bf16[3,2,64,128]...) custom-call(s32[2,26]{1,0:T(2,128)S(1)} %get-tuple-element.37.faces,, ...), custom_call_target="tpu_custom_call" | custom-call | flops 2000000000 | bytes 4194304 | tf_op jit(solution)/shard_map/conv0/pallas_call | solution.py:361
  12.5 8.3 %collective-permute-start.4 = (bf16[3,2,64,128]{3,2,1,0:T(8,128)(2,1)S(1)}, bf16[3,2,64,128]{3,2,1,0:T(8,128)(2,1)S(1)}, u32[]{:S(2)}, u32[]{:S(2)}) collective-permute-start(bf16[3,2,64,128]{3,2,1,0:T(8,128)(2,1)S(1)} %get-tuple-element.47), channel_id=1, source_target_pairs={{0,1},{1,0},{2,3},{3,2},{4,5},{5,4},{6,7},{7,6},{8,9},{9,8},{10,11... | collective-permute-start | bytes 294920 | tf_op jit(solution)/shard_map/ppermute | solution.py:283
  20.8 0.0 collective-permute-start.5
  20.9 1.8 %collective-permute-start.6 = (bf16[2,64,128]{2,1,0:T(8,128)(2,1)S(1)}, bf16[2,64,128]{2,1,0:T(8,128)(2,1)S(1)}, u32[]{:S(2)}, u32[]{:S(2)}) collective-permute-start(bf16[2,64,128]{2,1,0:T(8,128)(2,1)S(1)} %get-tuple-element.49), channel_id=1, source_target_pairs={{0,64},{64,0},{128,192},{192,128},{1,65},{65,1},{129,193},{193,129... | collective-permute-start | bytes 98312 | tf_op jit(solution)/shard_map/ppermute | solution.py:283
  22.6 0.3 collective-permute-start.7
  22.9 1.0 collective-permute-done.6.slab_a
  23.9 1.5 %collective-permute-done.7.slab_b = bf16[2,64,128]{2,1,0:T(8,128)(2,1)S(1)} collective-permute-done((bf16[2,64,128]{2,1,0:T(8,128)(2,1)S(1)}, bf16[2,64,128]{2,1,0:T(8,128)(2,1)S(1)}, u32[]{:S(2)}, u32[]{:S(2)}) %collective-permute-start.7) | collective-permute-done | bytes 32800 | tf_op jit(solution)/shard_map/ppermute | solution.py:283
  25.4 0.0 collective-permute-done.4.core
  25.4 0.0 collective-permute-done.5.rng
  25.4 0.0 copy-done
  25.4 4.4 %conv1.1 = (bf16[2,512,128]{2,1,0:T(8,128)(2,1)S(1)}, bf16[3,2,64,128]{3,2,1,0:T(8,128)(2,1)S(1)}, bf16[3,2,64,128]{3,2,1,0:T(8,128)(2,1)S(1)}, bf16[3,2,64,128]...) custom-call(s32[2,26]{1,0:T(2,128)S(1)} %get-tuple-element.37.faces,, ...), custom_call_target="tpu_custom_call" | custom-call | flops 2000000000 | bytes 4194304 | tf_op jit(solution)/shard_map/conv1/pallas_call | solution.py:361
  29.8 3.0 %collective-permute-start.8 = (bf16[3,2,64,128]{3,2,1,0:T(8,128)(2,1)S(1)}, bf16[3,2,64,128]{3,2,1,0:T(8,128)(2,1)S(1)}, u32[]{:S(2)}, u32[]{:S(2)}) collective-permute-start(bf16[3,2,64,128]{3,2,1,0:T(8,128)(2,1)S(1)} %get-tuple-element.54), channel_id=1, source_target_pairs={{0,1},{1,0},{2,3},{3,2},{4,5},{5,4},{6,7},{7,6},{8,9},{9,8},{10,11... | collective-permute-start | bytes 294920 | tf_op jit(solution)/shard_map/ppermute | solution.py:283
  32.8 0.4 collective-permute-start.9
  33.1 1.4 %collective-permute-start.10 = (bf16[2,64,128]{2,1,0:T(8,128)(2,1)S(1)}, bf16[2,64,128]{2,1,0:T(8,128)(2,1)S(1)}, u32[]{:S(2)}, u32[]{:S(2)}) collective-permute-start(bf16[2,64,128]{2,1,0:T(8,128)(2,1)S(1)} %get-tuple-element.56), channel_id=1, source_target_pairs={{0,64},{64,0},{128,192},{192,128},{1,65},{65,1},{129,193},{193,129... | collective-permute-start | bytes 98312 | tf_op jit(solution)/shard_map/ppermute | solution.py:283
  34.5 0.3 collective-permute-start.11
  34.8 1.1 collective-permute-done.10.slab_a
  35.9 1.4 %collective-permute-done.11.slab_b = bf16[2,64,128]{2,1,0:T(8,128)(2,1)S(1)} collective-permute-done((bf16[2,64,128]{2,1,0:T(8,128)(2,1)S(1)}, bf16[2,64,128]{2,1,0:T(8,128)(2,1)S(1)}, u32[]{:S(2)}, u32[]{:S(2)}) %collective-permute-start.11) | collective-permute-done | bytes 32800 | tf_op jit(solution)/shard_map/ppermute | solution.py:283
  37.3 0.0 collective-permute-done.8.core
  37.3 0.0 collective-permute-done.9.rng
  37.3 4.3 %conv2.1 = (bf16[2,512,128]{2,1,0:T(8,128)(2,1)S(1)}, bf16[3,2,64,128]{3,2,1,0:T(8,128)(2,1)S(1)}, bf16[3,2,64,128]{3,2,1,0:T(8,128)(2,1)S(1)}, bf16[3,2,64,128]...) custom-call(s32[2,26]{1,0:T(2,128)S(1)} %get-tuple-element.37.faces,, ...), custom_call_target="tpu_custom_call" | custom-call | flops 2000000000 | bytes 4194304 | tf_op jit(solution)/shard_map/conv2/pallas_call | solution.py:361
  41.6 3.3 %collective-permute-start.12 = (bf16[3,2,64,128]{3,2,1,0:T(8,128)(2,1)S(1)}, bf16[3,2,64,128]{3,2,1,0:T(8,128)(2,1)S(1)}, u32[]{:S(2)}, u32[]{:S(2)}) collective-permute-start(bf16[3,2,64,128]{3,2,1,0:T(8,128)(2,1)S(1)} %get-tuple-element.61), channel_id=1, source_target_pairs={{0,1},{1,0},{2,3},{3,2},{4,5},{5,4},{6,7},{7,6},{8,9},{9,8},{10,11... | collective-permute-start | bytes 294920 | tf_op jit(solution)/shard_map/ppermute | solution.py:283
  45.0 0.0 collective-permute-start.13
  45.0 1.4 %collective-permute-start.14 = (bf16[2,64,128]{2,1,0:T(8,128)(2,1)S(1)}, bf16[2,64,128]{2,1,0:T(8,128)(2,1)S(1)}, u32[]{:S(2)}, u32[]{:S(2)}) collective-permute-start(bf16[2,64,128]{2,1,0:T(8,128)(2,1)S(1)} %get-tuple-element.63), channel_id=1, source_target_pairs={{0,64},{64,0},{128,192},{192,128},{1,65},{65,1},{129,193},{193,129... | collective-permute-start | bytes 98312 | tf_op jit(solution)/shard_map/ppermute | solution.py:283
  46.4 0.3 collective-permute-start.15
  46.7 1.1 collective-permute-done.14.slab_a
  47.8 1.4 %collective-permute-done.15.slab_b = bf16[2,64,128]{2,1,0:T(8,128)(2,1)S(1)} collective-permute-done((bf16[2,64,128]{2,1,0:T(8,128)(2,1)S(1)}, bf16[2,64,128]{2,1,0:T(8,128)(2,1)S(1)}, u32[]{:S(2)}, u32[]{:S(2)}) %collective-permute-start.15) | collective-permute-done | bytes 32800 | tf_op jit(solution)/shard_map/ppermute | solution.py:283
  49.2 0.0 collective-permute-done.12.core
  49.2 0.0 collective-permute-done.13.rng
  49.2 3.9 %conv3.1 = bf16[128,64,128]{2,1,0:T(8,128)(2,1)S(1)} custom-call(s32[2,26]{1,0:T(2,128)S(1)} %get-tuple-element.37.faces, bf16[2,512,128]{2,1,0:T(8,128)(2,1)S(1)} %get-tuple-element.58.act, bf16[3,2,64,128]{3,2,1,0:T(8,128)(2,1)S(1)} %get-tuple-element.59.last, bf16[3,2,64,128]{3,2,1,0:T(8,128)(2,1)S(1)} %get-tuple-element.60.first, ...), custom_call_target="tpu_custom_call" | custom-call | flops 2000000000 | bytes 4194304 | tf_op jit(solution)/shard_map/conv3/pallas_call | solution.py:361
  53.1 0.0 copy-start.1
  53.1 58.1 %all_to_all.5.octants = bf16[128,64,128]{2,1,0:T(8,128)(2,1)S(1)} all-to-all(bf16[128,64,128]{2,1,0:T(8,128)(2,1)S(1)} %conv3.1), channel_id=1, replica_groups=mesh['slab'=4,'range'=64] {'range'}, dimensions={0} | all-to-all | bytes 4194304 | tf_op jit(solution)/shard_map/all_to_all | solution.py:384
  111.2 0.0 copy-done.1
  111.2 4.7 %grow.1 = bf16[128,64,512]{2,1,0:T(8,128)(2,1)} custom-call(bf16[128,64,128]{2,1,0:T(8,128)(2,1)S(1)} %all_to_all.5.octants, bf16[128,512]{1,0:T(8,128)(2,1)S(1)} %copy-done.1), custom_call_target="tpu_custom_call" | custom-call | tf_op jit(solution)/shard_map/grow/pallas_call | solution.py:386
Async XLA Ops:
  2.1 6.1 %collective-permute-start = (bf16[3,2,64,128]{3,2,1,0:T(8,128)(2,1)S(1)}, bf16[3,2,64,128]{3,2,1,0:T(8,128)(2,1)S(1)}, u32[]{:S(2)}, u32[]{:S(2)}) collective-permute-start(bf16[3,2,64,128]{3,2,1,0:T(8,128)(2,1)S(1)} %get-tuple-element.40), channel_id=1, source_target_pairs={{0,1},{1,0},{2,3},{3,2},{4,5},{5,4},{6,7},{7,6},{8,9},{9,8},{10,11... | collective-permute-start | bytes 294920 | tf_op jit(solution)/shard_map/ppermute | solution.py:283
  2.9 5.3 %collective-permute-start.1 = (bf16[3,2,64,128]{3,2,1,0:T(8,128)(2,1)S(1)}, bf16[3,2,64,128]{3,2,1,0:T(8,128)(2,1)S(1)}, u32[]{:S(2)}, u32[]{:S(2)}) collective-permute-start(bf16[3,2,64,128]{3,2,1,0:T(8,128)(2,1)S(1)} %get-tuple-element.41), channel_id=1, source_target_pairs={{0,63},{1,2},{2,1},{3,4},{4,3},{5,6},{6,5},{7,8},{8,7},{9,10},{10,... | collective-permute-start | bytes 294920 | tf_op jit(solution)/shard_map/ppermute | solution.py:283
  4.5 3.0 %collective-permute-start.2 = (bf16[2,64,128]{2,1,0:T(8,128)(2,1)S(1)}, bf16[2,64,128]{2,1,0:T(8,128)(2,1)S(1)}, u32[]{:S(2)}, u32[]{:S(2)}) collective-permute-start(bf16[2,64,128]{2,1,0:T(8,128)(2,1)S(1)} %get-tuple-element.42), channel_id=1, source_target_pairs={{0,64},{64,0},{128,192},{192,128},{1,65},{65,1},{129,193},{193,129... | collective-permute-start | bytes 98312 | tf_op jit(solution)/shard_map/ppermute | solution.py:283
  5.4 2.8 %collective-permute-start.3 = (bf16[2,64,128]{2,1,0:T(8,128)(2,1)S(1)}, bf16[2,64,128]{2,1,0:T(8,128)(2,1)S(1)}, u32[]{:S(2)}, u32[]{:S(2)}) collective-permute-start(bf16[2,64,128]{2,1,0:T(8,128)(2,1)S(1)} %get-tuple-element.43), channel_id=1, source_target_pairs={{0,192},{64,128},{128,64},{192,0},{1,193},{65,129},{129,65},{193,1... | collective-permute-start | bytes 98312 | tf_op jit(solution)/shard_map/ppermute | solution.py:283
  8.2 17.2 %copy-start = (bf16[2,512,128]{2,1,0:T(8,128)(2,1)S(1)}, bf16[2,512,128]{2,1,0:T(8,128)(2,1)}, u32[]{:S(2)}) copy-start(bf16[2,512,128]{2,1,0:T(8,128)(2,1)} %rest_0_.1) | copy-start | bytes 786436
  12.5 12.8 %collective-permute-start.4 = (bf16[3,2,64,128]{3,2,1,0:T(8,128)(2,1)S(1)}, bf16[3,2,64,128]{3,2,1,0:T(8,128)(2,1)S(1)}, u32[]{:S(2)}, u32[]{:S(2)}) collective-permute-start(bf16[3,2,64,128]{3,2,1,0:T(8,128)(2,1)S(1)} %get-tuple-element.47), channel_id=1, source_target_pairs={{0,1},{1,0},{2,3},{3,2},{4,5},{5,4},{6,7},{7,6},{8,9},{9,8},{10,11... | collective-permute-start | bytes 294920 | tf_op jit(solution)/shard_map/ppermute | solution.py:283
  20.8 4.5 %collective-permute-start.5 = (bf16[3,2,64,128]{3,2,1,0:T(8,128)(2,1)S(1)}, bf16[3,2,64,128]{3,2,1,0:T(8,128)(2,1)S(1)}, u32[]{:S(2)}, u32[]{:S(2)}) collective-permute-start(bf16[3,2,64,128]{3,2,1,0:T(8,128)(2,1)S(1)} %get-tuple-element.48), channel_id=1, source_target_pairs={{0,63},{1,2},{2,1},{3,4},{4,3},{5,6},{6,5},{7,8},{8,7},{9,10},{10,... | collective-permute-start | bytes 294920 | tf_op jit(solution)/shard_map/ppermute | solution.py:283
  20.9 3.1 %collective-permute-start.6 = (bf16[2,64,128]{2,1,0:T(8,128)(2,1)S(1)}, bf16[2,64,128]{2,1,0:T(8,128)(2,1)S(1)}, u32[]{:S(2)}, u32[]{:S(2)}) collective-permute-start(bf16[2,64,128]{2,1,0:T(8,128)(2,1)S(1)} %get-tuple-element.49), channel_id=1, source_target_pairs={{0,64},{64,0},{128,192},{192,128},{1,65},{65,1},{129,193},{193,129... | collective-permute-start | bytes 98312 | tf_op jit(solution)/shard_map/ppermute | solution.py:283
  22.6 2.8 %collective-permute-start.7 = (bf16[2,64,128]{2,1,0:T(8,128)(2,1)S(1)}, bf16[2,64,128]{2,1,0:T(8,128)(2,1)S(1)}, u32[]{:S(2)}, u32[]{:S(2)}) collective-permute-start(bf16[2,64,128]{2,1,0:T(8,128)(2,1)S(1)} %get-tuple-element.50), channel_id=1, source_target_pairs={{0,192},{64,128},{128,64},{192,0},{1,193},{65,129},{129,65},{193,1... | collective-permute-start | bytes 98312 | tf_op jit(solution)/shard_map/ppermute | solution.py:283
  29.8 7.5 %collective-permute-start.8 = (bf16[3,2,64,128]{3,2,1,0:T(8,128)(2,1)S(1)}, bf16[3,2,64,128]{3,2,1,0:T(8,128)(2,1)S(1)}, u32[]{:S(2)}, u32[]{:S(2)}) collective-permute-start(bf16[3,2,64,128]{3,2,1,0:T(8,128)(2,1)S(1)} %get-tuple-element.54), channel_id=1, source_target_pairs={{0,1},{1,0},{2,3},{3,2},{4,5},{5,4},{6,7},{7,6},{8,9},{9,8},{10,11... | collective-permute-start | bytes 294920 | tf_op jit(solution)/shard_map/ppermute | solution.py:283
  32.8 4.5 %collective-permute-start.9 = (bf16[3,2,64,128]{3,2,1,0:T(8,128)(2,1)S(1)}, bf16[3,2,64,128]{3,2,1,0:T(8,128)(2,1)S(1)}, u32[]{:S(2)}, u32[]{:S(2)}) collective-permute-start(bf16[3,2,64,128]{3,2,1,0:T(8,128)(2,1)S(1)} %get-tuple-element.55), channel_id=1, source_target_pairs={{0,63},{1,2},{2,1},{3,4},{4,3},{5,6},{6,5},{7,8},{8,7},{9,10},{10,... | collective-permute-start | bytes 294920 | tf_op jit(solution)/shard_map/ppermute | solution.py:283
  33.1 2.8 %collective-permute-start.10 = (bf16[2,64,128]{2,1,0:T(8,128)(2,1)S(1)}, bf16[2,64,128]{2,1,0:T(8,128)(2,1)S(1)}, u32[]{:S(2)}, u32[]{:S(2)}) collective-permute-start(bf16[2,64,128]{2,1,0:T(8,128)(2,1)S(1)} %get-tuple-element.56), channel_id=1, source_target_pairs={{0,64},{64,0},{128,192},{192,128},{1,65},{65,1},{129,193},{193,129... | collective-permute-start | bytes 98312 | tf_op jit(solution)/shard_map/ppermute | solution.py:283
  34.5 2.8 %collective-permute-start.11 = (bf16[2,64,128]{2,1,0:T(8,128)(2,1)S(1)}, bf16[2,64,128]{2,1,0:T(8,128)(2,1)S(1)}, u32[]{:S(2)}, u32[]{:S(2)}) collective-permute-start(bf16[2,64,128]{2,1,0:T(8,128)(2,1)S(1)} %get-tuple-element.57), channel_id=1, source_target_pairs={{0,192},{64,128},{128,64},{192,0},{1,193},{65,129},{129,65},{193,1... | collective-permute-start | bytes 98312 | tf_op jit(solution)/shard_map/ppermute | solution.py:283
  41.6 7.6 %collective-permute-start.12 = (bf16[3,2,64,128]{3,2,1,0:T(8,128)(2,1)S(1)}, bf16[3,2,64,128]{3,2,1,0:T(8,128)(2,1)S(1)}, u32[]{:S(2)}, u32[]{:S(2)}) collective-permute-start(bf16[3,2,64,128]{3,2,1,0:T(8,128)(2,1)S(1)} %get-tuple-element.61), channel_id=1, source_target_pairs={{0,1},{1,0},{2,3},{3,2},{4,5},{5,4},{6,7},{7,6},{8,9},{9,8},{10,11... | collective-permute-start | bytes 294920 | tf_op jit(solution)/shard_map/ppermute | solution.py:283
  45.0 4.2 %collective-permute-start.13 = (bf16[3,2,64,128]{3,2,1,0:T(8,128)(2,1)S(1)}, bf16[3,2,64,128]{3,2,1,0:T(8,128)(2,1)S(1)}, u32[]{:S(2)}, u32[]{:S(2)}) collective-permute-start(bf16[3,2,64,128]{3,2,1,0:T(8,128)(2,1)S(1)} %get-tuple-element.62), channel_id=1, source_target_pairs={{0,63},{1,2},{2,1},{3,4},{4,3},{5,6},{6,5},{7,8},{8,7},{9,10},{10,... | collective-permute-start | bytes 294920 | tf_op jit(solution)/shard_map/ppermute | solution.py:283
  45.0 2.8 %collective-permute-start.14 = (bf16[2,64,128]{2,1,0:T(8,128)(2,1)S(1)}, bf16[2,64,128]{2,1,0:T(8,128)(2,1)S(1)}, u32[]{:S(2)}, u32[]{:S(2)}) collective-permute-start(bf16[2,64,128]{2,1,0:T(8,128)(2,1)S(1)} %get-tuple-element.63), channel_id=1, source_target_pairs={{0,64},{64,0},{128,192},{192,128},{1,65},{65,1},{129,193},{193,129... | collective-permute-start | bytes 98312 | tf_op jit(solution)/shard_map/ppermute | solution.py:283
  46.4 2.8 %collective-permute-start.15 = (bf16[2,64,128]{2,1,0:T(8,128)(2,1)S(1)}, bf16[2,64,128]{2,1,0:T(8,128)(2,1)S(1)}, u32[]{:S(2)}, u32[]{:S(2)}) collective-permute-start(bf16[2,64,128]{2,1,0:T(8,128)(2,1)S(1)} %get-tuple-element.64), channel_id=1, source_target_pairs={{0,192},{64,128},{128,64},{192,0},{1,193},{65,129},{129,65},{193,1... | collective-permute-start | bytes 98312 | tf_op jit(solution)/shard_map/ppermute | solution.py:283
  53.1 58.1 %copy-start.1 = (bf16[128,512]{1,0:T(8,128)(2,1)S(1)}, bf16[128,512]{1,0:T(8,128)(2,1)}, u32[]{:S(2)}) copy-start(bf16[128,512]{1,0:T(8,128)(2,1)} %up.1) | copy-start | bytes 393220

commit v2 on v1

--- a/solution.py
+++ b/solution.py
@@ -6,6 +6,7 @@
 from jax.experimental import pallas as pl
 from jax.experimental.pallas import tpu as pltpu
 from jax.sharding import PartitionSpec as P
+
 
 EDGE = 8
 CH = 128
@@ -52,7 +53,7 @@
     value = normalize(load, gain, shift)
     act_s[pl.ds(b * VOX, VOX)] = value.reshape(VOX, CH)
     act[b] = value.reshape(VOX, CH).astype(jnp.bfloat16)
-    last, first, to_core, to_range, to_a, to_b = sends
+    last, first, _, _, _, _ = sends
     base = b * VOX
     for x in range(EDGE):
         rows = pl.ds(x * EDGE, EDGE)
@@ -136,7 +137,7 @@
         slots[c] = jnp.where(keeps[c] == 1, slot, -1)
 
 
-def assemble(act, faces, planes, table, field, window):
+def gather_halos(faces, planes, table, field, halos):
     row = 0
     for plane in planes:
         whole = plane[...].astype(jnp.float32)
@@ -145,52 +146,73 @@
         row += count
     table[pl.ds(ZERO * FACE, FACE)] = jnp.zeros((FACE, CH), jnp.float32)
 
-    def cell(x, y, b):
-        return ((x * 10 + y) * BRICKS + b) * PITCH
-
-    for b in range(BRICKS):
-        for x in range(EDGE):
-            for y in range(EDGE):
-                tile = act[b, pl.ds((x * 8 + y) * 8, 8)].astype(jnp.float32)
-                field[pl.ds(cell(x + 1, y + 1, b) + 8, 8)] = tile
+    def cell(kind, side, i, b):
+        return (((kind * 2 + side) * 10 + i) * BRICKS + b) * PITCH
+
+    across = BRICKS * PITCH
+    for side in range(2):
+        for deep in (7, 16):
+            field[pl.ds(cell(2, side, 1, 0) + deep, 16, stride=PITCH)] = jnp.zeros((16, CH), jnp.float32)
+        for kind in (1, 2):
+            for i in (0, 9):
+                halos[kind, side, i] = jnp.zeros((BRICKS * EDGE, 3 * CH), jnp.bfloat16)
     for b in range(BRICKS):
         for k, (dx, dy, dz) in enumerate(DIRECTIONS):
             base = pl.multiple_of(faces[b, k], FACE)
             cut = lambda d: 7 if d < 0 else 0
             put = lambda d: 0 if d < 0 else 9
             deep = 7 if dz < 0 else 16
-            if dx != 0:
-                px = put(dx)
-                ys = range(EDGE) if dy == 0 else [None]
+            kind = 0 if dx != 0 else 1 if dy != 0 else 2
+            side = 0 if (dx, dy, dz)[kind] < 0 else 1
+            if kind == 0 and dy != 0:
+                there = cell(0, side, put(dy), b)
                 if dz == 0:
-                    for y in ys:
-                        sy, py = (y, y + 1) if dy == 0 else (cut(dy), put(dy))
-                        field[pl.ds(cell(px, py, b) + 8, 8)] = table[pl.ds(base + sy * 8, 8)]
-                elif dy == 0:
-                    column = table[pl.ds(base + cut(dz), 8, stride=8)]
-                    field[pl.ds(cell(px, 1, b) + deep, 8, stride=BRICKS * PITCH)] = column
+                    field[pl.ds(there + 8, 8)] = table[pl.ds(base + cut(dy) * 8, 8)]
                 else:
-                    corner = table[pl.ds(base + cut(dy) * 8 + cut(dz), 1)]
-                    field[pl.ds(cell(px, put(dy), b) + deep, 1)] = corner
-            elif dy != 0:
-                py = put(dy)
-                if dz == 0:
-                    for x in range(EDGE):
-                        field[pl.ds(cell(x + 1, py, b) + 8, 8)] = table[pl.ds(base + x * 8, 8)]
-                else:
-                    column = table[pl.ds(base + cut(dz), 8, stride=8)]
-                    field[pl.ds(cell(1, py, b) + deep, 8, stride=10 * BRICKS * PITCH)] = column
+                    field[pl.ds(there + deep, 1)] = table[pl.ds(base + cut(dy) * 8 + cut(dz), 1)]
+            elif kind < 2 and dz != 0:
+                column = table[pl.ds(base + cut(dz), 8, stride=8)]
+                field[pl.ds(cell(kind, side, 1, b) + deep, 8, stride=across)] = column
             else:
-                for x in range(EDGE):
-                    rows = table[pl.ds(base + x * 8, 8)]
-                    field[pl.ds(cell(x + 1, 1, b) + deep, 8, stride=BRICKS * PITCH)] = rows
-    for x in range(10):
-        for y in range(10):
-            for w in range(3):
-                tile = jnp.concatenate(
-                    [field[pl.ds(cell(x, y, b) + 7 + w, 8)] for b in range(BRICKS)], axis=0
-                )
-                window[x, y, :, w * CH : (w + 1) * CH] = tile.astype(jnp.bfloat16)
+                for i in range(EDGE):
+                    field[pl.ds(cell(kind, side, i + 1, b) + 8, 8)] = table[pl.ds(base + i * 8, 8)]
+    for kind in range(3):
+        for side in range(2):
+            for i in range(10) if kind == 0 else range(1, 9):
+                for w in range(3):
+                    tile = jnp.concatenate(
+                        [field[pl.ds(cell(kind, side, i, b) + 7 + w, 8)] for b in range(BRICKS)], axis=0
+                    )
+                    halos[kind, side, i, :, w * CH : (w + 1) * CH] = tile.astype(jnp.bfloat16)
+
+
+def add_halos(halos, weights, acc):
+    rows = EDGE * BRICKS * EDGE
+    for kind in range(3):
+        wide = jnp.concatenate([halos[kind, :, s : s + 8] for s in range(3)], axis=-1)
+        sides = []
+        for near in (0, 2):
+            taps = []
+            for s in range(3):
+                for w in range(3):
+                    tap = [(near * 3 + s) * 3 + w, (s * 3 + near) * 3 + w, (s * 3 + w) * 3 + near][kind]
+                    taps.append(weights[pl.ds(tap * CH, CH)])
+            sides.append(jnp.concatenate(taps, axis=0))
+        part = jnp.dot(
+            wide.reshape(2 * rows, 9 * CH), jnp.concatenate(sides, axis=1), preferred_element_type=jnp.float32
+        )
+        for side, edge in ((0, 0), (1, 7)):
+            own = part[side * rows : (side + 1) * rows, side * CH : (side + 1) * CH]
+            if kind == 0:
+                acc[pl.ds(edge * rows, rows)] += own
+                continue
+            for x in range(EDGE):
+                if kind == 1:
+                    acc[pl.ds(x * rows + edge * 16, 16)] += own[x * 16 : x * 16 + 16]
+                    continue
+                for b in range(BRICKS):
+                    line = pl.ds(x * rows + b * 8 + edge, 8, stride=16)
+                    acc[line] = acc[line] + own[(x * 2 + b) * 8 : (x * 2 + b) * 8 + 8]
 
 
 def convolve(window, weights, total):
@@ -207,8 +229,30 @@
             total[...] += part
 
 
+def inner_kernel(step, act, weights_hbm, total, weights, window, sems):
+    copies = fetch(sems, (weights_hbm.at[step], weights))
+    blank = jnp.zeros((BRICKS * EDGE, 3 * CH), jnp.bfloat16)
+    row = lax.broadcasted_iota(jnp.int32, (EDGE, CH), 0)
+    for x in range(10):
+        for y in range(10):
+            if not (0 < x < 9 and 0 < y < 9):
+                window[x, y] = blank
+                continue
+            here = pl.ds(((x - 1) * 8 + y - 1) * 8, 8)
+            tiles = [act[b, here].astype(jnp.float32) for b in range(BRICKS)]
+            shifts = (
+                [jnp.where(row > 0, pltpu.roll(t, 1, 0), 0.0) for t in tiles],
+                tiles,
+                [jnp.where(row < 7, pltpu.roll(t, 7, 0), 0.0) for t in tiles],
+            )
+            for w in range(3):
+                window[x, y, :, w * CH : (w + 1) * CH] = jnp.concatenate(shifts[w], axis=0).astype(jnp.bfloat16)
+    copies[0].wait()
+    convolve(window, weights, total)
+
+
 def conv_kernel(
-    step, faces, act, last, first, core, rng, slab_a, slab_b, weights_hbm, gain_hbm, shift_hbm, *rest,
+    step, faces, last, first, core, rng, slab_a, slab_b, total, weights, gain_hbm, shift_hbm, *rest,
 ):
     rest = list(rest)
     state = rest.pop(0) if step % 2 else None
@@ -219,28 +263,25 @@
         act_out = rest.pop(0)
         sends = [rest.pop(0) for _ in range(6)]
         state_out = rest.pop(0) if step == 1 else None
-    table, field, window, weights, total, act_s, gain, shift, sems = rest
-    pairs = [(weights_hbm.at[step], weights)]
-    if step < 3:
-        pairs += [(gain_hbm, gain), (shift_hbm, shift)]
-    copies = fetch(sems, *pairs)
-    assemble(act, faces, (last, first, core, rng, slab_a, slab_b), table, field, window)
+    table, field, halos, acc, result, act_s, gain, shift, sems = rest
+    copies = fetch(sems, (gain_hbm, gain), (shift_hbm, shift)) if step < 3 else []
+    gather_halos(faces, (last, first, core, rng, slab_a, slab_b), table, field, halos)
+    acc[...] = total[...].reshape(BRICKS * VOX, CH)
+    add_halos(halos, weights, acc)
     if step == 3:
         packed[...] = jnp.zeros(packed.shape, packed.dtype)
     for copy in copies:
         copy.wait()
-    convolve(window, weights, total)
     for b in range(BRICKS):
+        value = acc[...].reshape(OCT, BRICKS, EDGE, CH)[:, b]
         if step % 2:
-            value = total[:, b] + state[b].astype(jnp.float32).reshape(OCT, EDGE, CH)
-            value = value.astype(jnp.bfloat16)
-            if step == 1:
-                state_out[b] = value.reshape(VOX, CH)
-            total[:, b] = value.astype(jnp.float32)
-        else:
-            total[:, b] = total[:, b].astype(jnp.bfloat16).astype(jnp.float32)
+            value = value + state[b].astype(jnp.float32).reshape(OCT, EDGE, CH)
+        value = value.astype(jnp.bfloat16)
+        if step == 1:
+            state_out[b] = value.reshape(VOX, CH)
+        result[b] = value.astype(jnp.float32)
         if step < 3:
-            load = lambda b=b: total[:, b]
+            load = lambda b=b: result[b]
             emit_active(load, b, gain[step + 1 : step + 2], shift[step + 1 : step + 2], act_s, act_out, sends)
     if step < 3:
         choose_sends(sends)
@@ -249,7 +290,7 @@
     for b in range(BRICKS):
         for ox in range(2):
             for oy in range(2):
-                tiles = total[pl.ds(ox * 32, 32), b].reshape(4, 8, EDGE, CH)
+                tiles = result[b, pl.ds(ox * 32, 32)].reshape(4, 8, EDGE, CH)
                 tiles = tiles[:, oy * 4 : oy * 4 + 4].reshape(4, 2, 2, EDGE, CH)
                 even, odd = tiles[:, :, 0], tiles[:, :, 1]
                 turn = lambda v: pltpu.roll(v.reshape(8, EDGE, CH), 4, 1).reshape(4, 2, EDGE, CH)
@@ -285,14 +326,11 @@
 
 def exchange(sends):
     last, first, to_core, to_range, to_a, to_b = sends
-    return (
-        last,
-        first,
-        swap(to_core, "range", False),
-        swap(to_range, "range", True),
-        swap(to_a, "slab", False),
-        swap(to_b, "slab", True),
-    )
+    rng = swap(to_range, "range", True)
+    slab_b = swap(to_b, "slab", True)
+    slab_a = swap(to_a, "slab", False)
+    core = swap(to_core, "range", False)
+    return last, first, core, rng, slab_a, slab_b
 
 
 SENDS = [
@@ -341,12 +379,24 @@
         cost_estimate=pl.CostEstimate(flops=1000, bytes_accessed=4096, transcendentals=0),
         name="route",
     )(in_hbm(neighbours), in_hbm(keep_mask), in_hbm(owner), act)
-    weights = in_hbm(conv_weights.reshape(4, 27 * CH, CH))
+    all_weights = in_hbm(conv_weights.reshape(4, 27 * CH, CH))
     state = features
     for step in range(4):
         planes = exchange(sends)
-        inputs = [faces, act, *planes, weights, gain, shift]
-        in_specs = [SMEM] + [VMEM] * 7 + [HBM] * 3
+        total, weights = pl.pallas_call(
+            functools.partial(inner_kernel, step),
+            out_shape=[jax.ShapeDtypeStruct((OCT, BRICKS, EDGE, CH), jnp.float32), bf16(27 * CH, CH)],
+            in_specs=[VMEM, HBM],
+            out_specs=[VMEM, VMEM],
+            scratch_shapes=[
+                pltpu.VMEM((10, 10, BRICKS * EDGE, 3 * CH), jnp.bfloat16),
+                pltpu.SemaphoreType.DMA((1,)),
+            ],
+            compiler_params=pltpu.CompilerParams(vmem_limit_bytes=LIMIT),
+            cost_estimate=pl.CostEstimate(flops=2 * 10**9, bytes_accessed=2**21, transcendentals=0),
+        )(act, all_weights)
+        inputs = [faces, *planes, total, weights, gain, shift]
+        in_specs = [SMEM] + [VMEM] * 8 + [HBM] * 2
         if step % 2:
             inputs.append(state)
             in_specs.append(VMEM)
@@ -365,17 +415,16 @@
             out_specs=[VMEM] * len(outs),
             scratch_shapes=[
                 pltpu.VMEM((FACES * FACE, CH), jnp.float32),
-                pltpu.VMEM((100 * BRICKS * PITCH, CH), jnp.float32),
-                pltpu.VMEM((10, 10, BRICKS * EDGE, 3 * CH), jnp.bfloat16),
-                pltpu.VMEM((27 * CH, CH), jnp.bfloat16),
-                pltpu.VMEM((OCT, BRICKS, EDGE, CH), jnp.float32),
+                pltpu.VMEM((6 * 10 * BRICKS * PITCH, CH), jnp.float32),
+                pltpu.VMEM((3, 2, 10, BRICKS * EDGE, 3 * CH), jnp.bfloat16),
+                pltpu.VMEM((BRICKS * VOX, CH), jnp.float32),
+                pltpu.VMEM((BRICKS, OCT, EDGE, CH), jnp.float32),
                 act_s,
                 *norm_s,
-                pltpu.SemaphoreType.DMA((3,)),
+                pltpu.SemaphoreType.DMA((2,)),
             ],
             compiler_params=pltpu.CompilerParams(vmem_limit_bytes=LIMIT),
-            cost_estimate=pl.CostEstimate(flops=2 * 10**9, bytes_accessed=2**22, transcendentals=2**17),
-            name=f"conv{step}",
+            cost_estimate=pl.CostEstimate(flops=5 * 10**8, bytes_accessed=2**22, transcendentals=2**17),
         )(*inputs)
         if step < 3:
             act, sends = result[0], result[1:7]

time: 118 us -> 118 us (level)
  waiting for transfers between devices: 8.24 us -> 2.42 us
  Pallas kernels: 25.7 us -> 30.4 us
  starting transfers between devices: 23.7 us -> 25.4 us
    pallas_call x0 -> x4, Pallas kernels: none -> 12.8 us  [shards(): pl.pallas_call(functools.partial(inner_kernel, step), out_shape=[jax.Shap...]
    pallas_call x4, Pallas kernels: 16.9 us -> 8.73 us  [shards(): pl.pallas_call(functools.partial(conv_kernel, step), out_shape=outs, in_s...]
    ppermute x16, waiting for transfers between devices: 8.24 us -> 2.42 us  [swap(): return lax.ppermute(block, axis, route)]
    ppermute x16, starting transfers between devices: 23.7 us -> 25.4 us  [swap(): return lax.ppermute(block, axis, route)]
  transfers between devices with their start and end apart: 16 -> 16, of which waited for: 7 -> 3; matrix products, arithmetic and copies ran while one was open for 0% -> 0% of each run, Pallas kernels for 2% -> 13%
where the time goes in v2:
time: 118 us; the launch traced here: 116 us
  blocking collectives  57.9 us (49%)
  Pallas kernels  30.4 us (26%)
  starting transfers between devices  25.4 us (22%)
  waiting for transfers between devices  2.42 us (2%)
    all_to_all x1, blocking collectives, shards(): lax.all_to_all(result[0], 'range', split_axis=0, concat_axis=0, tiled=True)  57.9 us
    ppermute x16, starting transfers between devices, swap(): return lax.ppermute(block, axis, route)  25.4 us
    pallas_call x4, Pallas kernels, shards(): pl.pallas_call(functools.partial(inner_kernel, step), out_shape=[jax.Shap...  12.8 us
    pallas_call x4, Pallas kernels, shards(): pl.pallas_call(functools.partial(conv_kernel, step), out_shape=outs, in_s...  8.73 us
    pallas_call x1, Pallas kernels, shards(): pl.pallas_call(grow_kernel, grid=(128 // slab,), out_shape=bf16(128, OCT,...  4.73 us
    ppermute x16, waiting for transfers between devices, swap(): return lax.ppermute(block, axis, route)  2.42 us
  transfers between devices with their start and end apart: 16, of which 3 were waited for; matrix products, arithmetic and copies ran while one was open for 0% of the time, Pallas kernels for 13%

profile of v2, /device:TPU:5, one launch (start us, length us, event | category | flops | bytes accessed | tf_op | source)
XLA Modules:
  0.0 116.4 jit_solution(4785915805989708384)
XLA Ops:
  0.0 2.1 %start.1 = (bf16[2,512,128]{2,1,0:T(8,128)(2,1)S(1)}, bf16[3,2,64,128]{3,2,1,0:T(8,128)(2,1)S(1)}, bf16[3,2,64,128]{3,2,1,0:T(8,128)(2,1)S(1)}, bf16[3,2,64,128]...) custom-call(bf16[2,512,128]{2,1,0:T(8,128)(2,1)} %rest_0_.1, ...), custom_call_target="tpu_custom_call" | custom-call | flops 10000000 | bytes 4194304 | tf_op jit(solution)/shard_map/start/pallas_call | solution.py:352
  2.1 1.0 collective-permute-start.2
  3.1 0.0 collective-permute-start.3
  3.1 2.5 %collective-permute-start = (bf16[3,2,64,128]{3,2,1,0:T(8,128)(2,1)S(1)}, bf16[3,2,64,128]{3,2,1,0:T(8,128)(2,1)S(1)}, u32[]{:S(2)}, u32[]{:S(2)}) collective-permute-start(bf16[3,2,64,128]{3,2,1,0:T(8,128)(2,1)S(1)} %get-tuple-element.48), channel_id=1, source_target_pairs={{0,1},{1,0},{2,3},{3,2},{4,5},{5,4},{6,7},{7,6},{8,9},{9,8},{10,11... | collective-permute-start | bytes 294920 | tf_op jit(solution)/shard_map/ppermute | solution.py:324
  5.6 0.0 collective-permute-start.1
  5.6 3.2 %shard_map.82 = (f32[64,2,8,128]{3,2,1,0:T(8,128)S(1)}, bf16[3456,128]{1,0:T(8,128)(2,1)S(1)}) custom-call(bf16[2,512,128]{2,1,0:T(8,128)(2,1)S(1)} %get-tuple-element.44.after.act, bf16[4,3456,128]{2,1,0:T(8,128)(2,1)} %bitcast.1), custom_call_target="tpu_custom_call" | custom-call | flops 2000000000 | bytes 2097152 | tf_op jit(solution)/shard_map/pallas_call | solution.py:386
  8.8 2.1 %route.1 = (s32[2,26]{1,0:T(2,128)S(1)}, s32[16]{0:T(128)S(1)}) custom-call(s32[2,26]{1,0:T(2,128)} %neighbours_hbm.1, s32[2,8]{1,0:T(2,128)} %kept_hbm.1, s32[2,8]{1,0:T(2,128)} %owner_hbm.1, bf16[2,512,128]{2,1,0:T(8,128)(2,1)S(1)} %get-tuple-element.44.after.act), custom_call_target="tpu_custom_call" | custom-call | flops 1000 | bytes 4096 | tf_op jit(solution)/shard_map/route/pallas_call | solution.py:367
  10.9 0.0 collective-permute-done.2.slab_a
  10.9 0.0 collective-permute-done.3.slab_b
  10.9 0.0 collective-permute-done.core
  10.9 0.0 collective-permute-done.1.rng
  11.0 2.2 %shard_map.83 = (bf16[2,512,128]{2,1,0:T(8,128)(2,1)S(1)}, bf16[3,2,64,128]{3,2,1,0:T(8,128)(2,1)S(1)}, bf16[3,2,64,128]{3,2,1,0:T(8,128)(2,1)S(1)}, bf16[3,2,64...) custom-call(s32[2,26]{1,0:T(2,128)S(1)} %get-tuple-element.45.faces,, ...), custom_call_target="tpu_custom_call" | custom-call | flops 500000000 | bytes 4194304 | tf_op jit(solution)/shard_map/pallas_call | solution.py:411
  13.2 1.7 %collective-permute-start.6 = (bf16[2,64,128]{2,1,0:T(8,128)(2,1)S(1)}, bf16[2,64,128]{2,1,0:T(8,128)(2,1)S(1)}, u32[]{:S(2)}, u32[]{:S(2)}) collective-permute-start(bf16[2,64,128]{2,1,0:T(8,128)(2,1)S(1)} %get-tuple-element.58), channel_id=1, source_target_pairs={{0,64},{64,0},{128,192},{192,128},{1,65},{65,1},{129,193},{193,129... | collective-permute-start | bytes 98312 | tf_op jit(solution)/shard_map/ppermute | solution.py:324
  14.9 1.2 %collective-permute-start.7 = (bf16[2,64,128]{2,1,0:T(8,128)(2,1)S(1)}, bf16[2,64,128]{2,1,0:T(8,128)(2,1)S(1)}, u32[]{:S(2)}, u32[]{:S(2)}) collective-permute-start(bf16[2,64,128]{2,1,0:T(8,128)(2,1)S(1)} %get-tuple-element.59), channel_id=1, source_target_pairs={{0,192},{64,128},{128,64},{192,0},{1,193},{65,129},{129,65},{193,1... | collective-permute-start | bytes 98312 | tf_op jit(solution)/shard_map/ppermute | solution.py:324
  16.1 7.5 %collective-permute-start.4 = (bf16[3,2,64,128]{3,2,1,0:T(8,128)(2,1)S(1)}, bf16[3,2,64,128]{3,2,1,0:T(8,128)(2,1)S(1)}, u32[]{:S(2)}, u32[]{:S(2)}) collective-permute-start(bf16[3,2,64,128]{3,2,1,0:T(8,128)(2,1)S(1)} %get-tuple-element.56), channel_id=1, source_target_pairs={{0,1},{1,0},{2,3},{3,2},{4,5},{5,4},{6,7},{7,6},{8,9},{9,8},{10,11... | collective-permute-start | bytes 294920 | tf_op jit(solution)/shard_map/ppermute | solution.py:324
  23.6 0.0 collective-permute-start.5
  23.6 0.0 copy-start
  23.6 3.2 %shard_map.84 = (f32[64,2,8,128]{3,2,1,0:T(8,128)S(1)}, bf16[3456,128]{1,0:T(8,128)(2,1)S(1)}) custom-call(bf16[2,512,128]{2,1,0:T(8,128)(2,1)S(1)} %get-tuple-element.60.act, bf16[4,3456,128]{2,1,0:T(8,128)(2,1)} %bitcast.2), custom_call_target="tpu_custom_call" | custom-call | flops 2000000000 | bytes 2097152 | tf_op jit(solution)/shard_map/pallas_call | solution.py:386
  26.8 0.0 collective-permute-done.6.slab_a
  26.9 0.0 collective-permute-done.7.slab_b
  26.9 0.0 collective-permute-done.4.core
  26.9 0.8 collective-permute-done.5.rng
  27.6 0.0 copy-done
  27.6 2.4 %shard_map.85 = (bf16[2,512,128]{2,1,0:T(8,128)(2,1)S(1)}, bf16[3,2,64,128]{3,2,1,0:T(8,128)(2,1)S(1)}, bf16[3,2,64,128]{3,2,1,0:T(8,128)(2,1)S(1)}, bf16[3,2,64...) custom-call(s32[2,26]{1,0:T(2,128)S(1)} %get-tuple-element.45.faces,, ...), custom_call_target="tpu_custom_call" | custom-call | flops 500000000 | bytes 4194304 | tf_op jit(solution)/shard_map/pallas_call | solution.py:411
  30.0 1.0 collective-permute-start.10
  31.0 0.0 collective-permute-start.11
  31.0 3.6 %collective-permute-start.8 = (bf16[3,2,64,128]{3,2,1,0:T(8,128)(2,1)S(1)}, bf16[3,2,64,128]{3,2,1,0:T(8,128)(2,1)S(1)}, u32[]{:S(2)}, u32[]{:S(2)}) collective-permute-start(bf16[3,2,64,128]{3,2,1,0:T(8,128)(2,1)S(1)} %get-tuple-element.65), channel_id=1, source_target_pairs={{0,1},{1,0},{2,3},{3,2},{4,5},{5,4},{6,7},{7,6},{8,9},{9,8},{10,11... | collective-permute-start | bytes 294920 | tf_op jit(solution)/shard_map/ppermute | solution.py:324
  34.7 0.0 collective-permute-start.9
  34.7 3.2 %shard_map.86 = (f32[64,2,8,128]{3,2,1,0:T(8,128)S(1)}, bf16[3456,128]{1,0:T(8,128)(2,1)S(1)}) custom-call(bf16[2,512,128]{2,1,0:T(8,128)(2,1)S(1)} %get-tuple-element.69.act, bf16[4,3456,128]{2,1,0:T(8,128)(2,1)} %bitcast.3), custom_call_target="tpu_custom_call" | custom-call | flops 2000000000 | bytes 2097152 | tf_op jit(solution)/shard_map/pallas_call | solution.py:386
  37.9 0.0 collective-permute-done.10.slab_a
  37.9 0.0 collective-permute-done.11.slab_b
  37.9 0.0 collective-permute-done.8.core
  37.9 0.8 collective-permute-done.9.rng
  38.7 2.2 %shard_map.87 = (bf16[2,512,128]{2,1,0:T(8,128)(2,1)S(1)}, bf16[3,2,64,128]{3,2,1,0:T(8,128)(2,1)S(1)}, bf16[3,2,64,128]{3,2,1,0:T(8,128)(2,1)S(1)}, bf16[3,2,64...) custom-call(s32[2,26]{1,0:T(2,128)S(1)} %get-tuple-element.45.faces,, ...), custom_call_target="tpu_custom_call" | custom-call | flops 500000000 | bytes 4194304 | tf_op jit(solution)/shard_map/pallas_call | solution.py:411
  41.0 1.7 %collective-permute-start.14 = (bf16[2,64,128]{2,1,0:T(8,128)(2,1)S(1)}, bf16[2,64,128]{2,1,0:T(8,128)(2,1)S(1)}, u32[]{:S(2)}, u32[]{:S(2)}) collective-permute-start(bf16[2,64,128]{2,1,0:T(8,128)(2,1)S(1)} %get-tuple-element.76), channel_id=1, source_target_pairs={{0,64},{64,0},{128,192},{192,128},{1,65},{65,1},{129,193},{193,129... | collective-permute-start | bytes 98312 | tf_op jit(solution)/shard_map/ppermute | solution.py:324
  42.7 1.2 %collective-permute-start.15 = (bf16[2,64,128]{2,1,0:T(8,128)(2,1)S(1)}, bf16[2,64,128]{2,1,0:T(8,128)(2,1)S(1)}, u32[]{:S(2)}, u32[]{:S(2)}) collective-permute-start(bf16[2,64,128]{2,1,0:T(8,128)(2,1)S(1)} %get-tuple-element.77), channel_id=1, source_target_pairs={{0,192},{64,128},{128,64},{192,0},{1,193},{65,129},{129,65},{193,1... | collective-permute-start | bytes 98312 | tf_op jit(solution)/shard_map/ppermute | solution.py:324
  43.9 3.9 %collective-permute-start.12 = (bf16[3,2,64,128]{3,2,1,0:T(8,128)(2,1)S(1)}, bf16[3,2,64,128]{3,2,1,0:T(8,128)(2,1)S(1)}, u32[]{:S(2)}, u32[]{:S(2)}) collective-permute-start(bf16[3,2,64,128]{3,2,1,0:T(8,128)(2,1)S(1)} %get-tuple-element.74), channel_id=1, source_target_pairs={{0,1},{1,0},{2,3},{3,2},{4,5},{5,4},{6,7},{7,6},{8,9},{9,8},{10,11... | collective-permute-start | bytes 294920 | tf_op jit(solution)/shard_map/ppermute | solution.py:324
  47.8 0.0 collective-permute-start.13
  47.8 3.2 %shard_map.88 = (f32[64,2,8,128]{3,2,1,0:T(8,128)S(1)}, bf16[3456,128]{1,0:T(8,128)(2,1)S(1)}) custom-call(bf16[2,512,128]{2,1,0:T(8,128)(2,1)S(1)} %get-tuple-element.78.act, bf16[4,3456,128]{2,1,0:T(8,128)(2,1)} %bitcast.4), custom_call_target="tpu_custom_call" | custom-call | flops 2000000000 | bytes 2097152 | tf_op jit(solution)/shard_map/pallas_call | solution.py:386
  51.0 0.0 collective-permute-done.14.slab_a
  51.0 0.0 collective-permute-done.15.slab_b
  51.0 0.0 collective-permute-done.12.core
  51.0 0.8 collective-permute-done.13.rng
  51.8 0.0 copy-start.1
  51.8 1.9 %shard_map.89 = bf16[128,64,128]{2,1,0:T(8,128)(2,1)S(1)} custom-call(s32[2,26]{1,0:T(2,128)S(1)} %get-tuple-element.45.faces, bf16[3,2,64,128]{3,2,1,0:T(8,128)(2,1)S(1)} %get-tuple-element.72.last, bf16[3,2,64,128]{3,2,1,0:T(8,128)(2,1)S(1)} %get-tuple-element.73.first, bf16[3,2,64,128]{3,2,1,0:T(8,128)(2,1)S(1)} %collective-permute-done.12.core, ...), custom_call_target="tpu_custom_call" | custom-call | flops 500000000 | bytes 4194304 | tf_op jit(solution)/shard_map/pallas_call | solution.py:411
  53.7 57.9 %all_to_all.5.octants = bf16[128,64,128]{2,1,0:T(8,128)(2,1)S(1)} all-to-all(bf16[128,64,128]{2,1,0:T(8,128)(2,1)S(1)} %shard_map.89), channel_id=1, replica_groups=mesh['slab'=4,'range'=64] {'range'}, dimensions={0} | all-to-all | bytes 4194304 | tf_op jit(solution)/shard_map/all_to_all | solution.py:433
  111.6 0.0 copy-done.1
  111.7 4.7 %grow.1 = bf16[128,64,512]{2,1,0:T(8,128)(2,1)} custom-call(bf16[128,64,128]{2,1,0:T(8,128)(2,1)S(1)} %all_to_all.5.octants, bf16[128,512]{1,0:T(8,128)(2,1)S(1)} %copy-done.1), custom_call_target="tpu_custom_call" | custom-call | tf_op jit(solution)/shard_map/grow/pallas_call | solution.py:435
Async XLA Ops:
  2.1 8.8 %collective-permute-start.2 = (bf16[2,64,128]{2,1,0:T(8,128)(2,1)S(1)}, bf16[2,64,128]{2,1,0:T(8,128)(2,1)S(1)}, u32[]{:S(2)}, u32[]{:S(2)}) collective-permute-start(bf16[2,64,128]{2,1,0:T(8,128)(2,1)S(1)} %get-tuple-element.50), channel_id=1, source_target_pairs={{0,64},{64,0},{128,192},{192,128},{1,65},{65,1},{129,193},{193,129... | collective-permute-start | bytes 98312 | tf_op jit(solution)/shard_map/ppermute | solution.py:324
  3.1 7.8 %collective-permute-start.3 = (bf16[2,64,128]{2,1,0:T(8,128)(2,1)S(1)}, bf16[2,64,128]{2,1,0:T(8,128)(2,1)S(1)}, u32[]{:S(2)}, u32[]{:S(2)}) collective-permute-start(bf16[2,64,128]{2,1,0:T(8,128)(2,1)S(1)} %get-tuple-element.51), channel_id=1, source_target_pairs={{0,192},{64,128},{128,64},{192,0},{1,193},{65,129},{129,65},{193,1... | collective-permute-start | bytes 98312 | tf_op jit(solution)/shard_map/ppermute | solution.py:324
  3.1 7.8 %collective-permute-start = (bf16[3,2,64,128]{3,2,1,0:T(8,128)(2,1)S(1)}, bf16[3,2,64,128]{3,2,1,0:T(8,128)(2,1)S(1)}, u32[]{:S(2)}, u32[]{:S(2)}) collective-permute-start(bf16[3,2,64,128]{3,2,1,0:T(8,128)(2,1)S(1)} %get-tuple-element.48), channel_id=1, source_target_pairs={{0,1},{1,0},{2,3},{3,2},{4,5},{5,4},{6,7},{7,6},{8,9},{9,8},{10,11... | collective-permute-start | bytes 294920 | tf_op jit(solution)/shard_map/ppermute | solution.py:324
  5.6 5.3 %collective-permute-start.1 = (bf16[3,2,64,128]{3,2,1,0:T(8,128)(2,1)S(1)}, bf16[3,2,64,128]{3,2,1,0:T(8,128)(2,1)S(1)}, u32[]{:S(2)}, u32[]{:S(2)}) collective-permute-start(bf16[3,2,64,128]{3,2,1,0:T(8,128)(2,1)S(1)} %get-tuple-element.49), channel_id=1, source_target_pairs={{0,63},{1,2},{2,1},{3,4},{4,3},{5,6},{6,5},{7,8},{8,7},{9,10},{10,... | collective-permute-start | bytes 294920 | tf_op jit(solution)/shard_map/ppermute | solution.py:324
  13.2 13.6 %collective-permute-start.6 = (bf16[2,64,128]{2,1,0:T(8,128)(2,1)S(1)}, bf16[2,64,128]{2,1,0:T(8,128)(2,1)S(1)}, u32[]{:S(2)}, u32[]{:S(2)}) collective-permute-start(bf16[2,64,128]{2,1,0:T(8,128)(2,1)S(1)} %get-tuple-element.58), channel_id=1, source_target_pairs={{0,64},{64,0},{128,192},{192,128},{1,65},{65,1},{129,193},{193,129... | collective-permute-start | bytes 98312 | tf_op jit(solution)/shard_map/ppermute | solution.py:324
  14.9 11.9 %collective-permute-start.7 = (bf16[2,64,128]{2,1,0:T(8,128)(2,1)S(1)}, bf16[2,64,128]{2,1,0:T(8,128)(2,1)S(1)}, u32[]{:S(2)}, u32[]{:S(2)}) collective-permute-start(bf16[2,64,128]{2,1,0:T(8,128)(2,1)S(1)} %get-tuple-element.59), channel_id=1, source_target_pairs={{0,192},{64,128},{128,64},{192,0},{1,193},{65,129},{129,65},{193,1... | collective-permute-start | bytes 98312 | tf_op jit(solution)/shard_map/ppermute | solution.py:324
  16.1 10.7 %collective-permute-start.4 = (bf16[3,2,64,128]{3,2,1,0:T(8,128)(2,1)S(1)}, bf16[3,2,64,128]{3,2,1,0:T(8,128)(2,1)S(1)}, u32[]{:S(2)}, u32[]{:S(2)}) collective-permute-start(bf16[3,2,64,128]{3,2,1,0:T(8,128)(2,1)S(1)} %get-tuple-element.56), channel_id=1, source_target_pairs={{0,1},{1,0},{2,3},{3,2},{4,5},{5,4},{6,7},{7,6},{8,9},{9,8},{10,11... | collective-permute-start | bytes 294920 | tf_op jit(solution)/shard_map/ppermute | solution.py:324
  23.6 4.0 %collective-permute-start.5 = (bf16[3,2,64,128]{3,2,1,0:T(8,128)(2,1)S(1)}, bf16[3,2,64,128]{3,2,1,0:T(8,128)(2,1)S(1)}, u32[]{:S(2)}, u32[]{:S(2)}) collective-permute-start(bf16[3,2,64,128]{3,2,1,0:T(8,128)(2,1)S(1)} %get-tuple-element.57), channel_id=1, source_target_pairs={{0,63},{1,2},{2,1},{3,4},{4,3},{5,6},{6,5},{7,8},{8,7},{9,10},{10,... | collective-permute-start | bytes 294920 | tf_op jit(solution)/shard_map/ppermute | solution.py:324
  23.6 4.0 %copy-start = (bf16[2,512,128]{2,1,0:T(8,128)(2,1)S(1)}, bf16[2,512,128]{2,1,0:T(8,128)(2,1)}, u32[]{:S(2)}) copy-start(bf16[2,512,128]{2,1,0:T(8,128)(2,1)} %rest_0_.1) | copy-start | bytes 786436
  30.0 7.8 %collective-permute-start.10 = (bf16[2,64,128]{2,1,0:T(8,128)(2,1)S(1)}, bf16[2,64,128]{2,1,0:T(8,128)(2,1)S(1)}, u32[]{:S(2)}, u32[]{:S(2)}) collective-permute-start(bf16[2,64,128]{2,1,0:T(8,128)(2,1)S(1)} %get-tuple-element.67), channel_id=1, source_target_pairs={{0,64},{64,0},{128,192},{192,128},{1,65},{65,1},{129,193},{193,129... | collective-permute-start | bytes 98312 | tf_op jit(solution)/shard_map/ppermute | solution.py:324
  31.0 6.9 %collective-permute-start.11 = (bf16[2,64,128]{2,1,0:T(8,128)(2,1)S(1)}, bf16[2,64,128]{2,1,0:T(8,128)(2,1)S(1)}, u32[]{:S(2)}, u32[]{:S(2)}) collective-permute-start(bf16[2,64,128]{2,1,0:T(8,128)(2,1)S(1)} %get-tuple-element.68), channel_id=1, source_target_pairs={{0,192},{64,128},{128,64},{192,0},{1,193},{65,129},{129,65},{193,1... | collective-permute-start | bytes 98312 | tf_op jit(solution)/shard_map/ppermute | solution.py:324
  31.0 6.9 %collective-permute-start.8 = (bf16[3,2,64,128]{3,2,1,0:T(8,128)(2,1)S(1)}, bf16[3,2,64,128]{3,2,1,0:T(8,128)(2,1)S(1)}, u32[]{:S(2)}, u32[]{:S(2)}) collective-permute-start(bf16[3,2,64,128]{3,2,1,0:T(8,128)(2,1)S(1)} %get-tuple-element.65), channel_id=1, source_target_pairs={{0,1},{1,0},{2,3},{3,2},{4,5},{5,4},{6,7},{7,6},{8,9},{9,8},{10,11... | collective-permute-start | bytes 294920 | tf_op jit(solution)/shard_map/ppermute | solution.py:324
  34.7 4.0 %collective-permute-start.9 = (bf16[3,2,64,128]{3,2,1,0:T(8,128)(2,1)S(1)}, bf16[3,2,64,128]{3,2,1,0:T(8,128)(2,1)S(1)}, u32[]{:S(2)}, u32[]{:S(2)}) collective-permute-start(bf16[3,2,64,128]{3,2,1,0:T(8,128)(2,1)S(1)} %get-tuple-element.66), channel_id=1, source_target_pairs={{0,63},{1,2},{2,1},{3,4},{4,3},{5,6},{6,5},{7,8},{8,7},{9,10},{10,... | collective-permute-start | bytes 294920 | tf_op jit(solution)/shard_map/ppermute | solution.py:324
  41.0 10.0 %collective-permute-start.14 = (bf16[2,64,128]{2,1,0:T(8,128)(2,1)S(1)}, bf16[2,64,128]{2,1,0:T(8,128)(2,1)S(1)}, u32[]{:S(2)}, u32[]{:S(2)}) collective-permute-start(bf16[2,64,128]{2,1,0:T(8,128)(2,1)S(1)} %get-tuple-element.76), channel_id=1, source_target_pairs={{0,64},{64,0},{128,192},{192,128},{1,65},{65,1},{129,193},{193,129... | collective-permute-start | bytes 98312 | tf_op jit(solution)/shard_map/ppermute | solution.py:324
  42.7 8.3 %collective-permute-start.15 = (bf16[2,64,128]{2,1,0:T(8,128)(2,1)S(1)}, bf16[2,64,128]{2,1,0:T(8,128)(2,1)S(1)}, u32[]{:S(2)}, u32[]{:S(2)}) collective-permute-start(bf16[2,64,128]{2,1,0:T(8,128)(2,1)S(1)} %get-tuple-element.77), channel_id=1, source_target_pairs={{0,192},{64,128},{128,64},{192,0},{1,193},{65,129},{129,65},{193,1... | collective-permute-start | bytes 98312 | tf_op jit(solution)/shard_map/ppermute | solution.py:324
  43.9 7.1 %collective-permute-start.12 = (bf16[3,2,64,128]{3,2,1,0:T(8,128)(2,1)S(1)}, bf16[3,2,64,128]{3,2,1,0:T(8,128)(2,1)S(1)}, u32[]{:S(2)}, u32[]{:S(2)}) collective-permute-start(bf16[3,2,64,128]{3,2,1,0:T(8,128)(2,1)S(1)} %get-tuple-element.74), channel_id=1, source_target_pairs={{0,1},{1,0},{2,3},{3,2},{4,5},{5,4},{6,7},{7,6},{8,9},{9,8},{10,11... | collective-permute-start | bytes 294920 | tf_op jit(solution)/shard_map/ppermute | solution.py:324
  47.8 4.0 %collective-permute-start.13 = (bf16[3,2,64,128]{3,2,1,0:T(8,128)(2,1)S(1)}, bf16[3,2,64,128]{3,2,1,0:T(8,128)(2,1)S(1)}, u32[]{:S(2)}, u32[]{:S(2)}) collective-permute-start(bf16[3,2,64,128]{3,2,1,0:T(8,128)(2,1)S(1)} %get-tuple-element.75), channel_id=1, source_target_pairs={{0,63},{1,2},{2,1},{3,4},{4,3},{5,6},{6,5},{7,8},{8,7},{9,10},{10,... | collective-permute-start | bytes 294920 | tf_op jit(solution)/shard_map/ppermute | solution.py:324
  51.8 59.8 %copy-start.1 = (bf16[128,512]{1,0:T(8,128)(2,1)S(1)}, bf16[128,512]{1,0:T(8,128)(2,1)}, u32[]{:S(2)}) copy-start(bf16[128,512]{1,0:T(8,128)(2,1)} %up.1) | copy-start | bytes 393220

commit v3 on v2

--- a/solution.py
+++ b/solution.py
@@ -27,7 +27,6 @@
 
 VMEM = pl.BlockSpec(memory_space=pltpu.VMEM)
 SMEM = pl.BlockSpec(memory_space=pltpu.SMEM)
-ANY = pl.BlockSpec(memory_space=pl.ANY)
 HBM = pl.BlockSpec(memory_space=pltpu.HBM)
 
 
@@ -107,9 +106,7 @@
     choose_sends(sends)
 
 
-def route_kernel(neighbours_hbm, kept_hbm, owner_hbm, after, faces, slots, neighbours, kept, owner, sems):
-    for copy in fetch(sems, (neighbours_hbm, neighbours), (kept_hbm, kept), (owner_hbm, owner)):
-        copy.wait()
+def find_routes(neighbours, kept, owner, faces, slots):
     odd_range, odd_slab = parity("range"), parity("slab")
     below = jnp.where(odd_range == 1, CORE, RANGE)
     above = jnp.where(odd_range == 1, RANGE, CORE)
@@ -120,10 +117,10 @@
             axis = [a for a in range(3) if offsets[a] != 0][0]
             negative = offsets[axis] < 0
             entry = neighbours[b, k]
-            source = entry // BRICKS
+            source = entry >> 1
             own, side, slab = (OWN_HI, below, under) if negative else (OWN_LO, above, over)
             near = jnp.where(source == 0, own, side) + axis * BRICKS
-            face = jnp.where(source > 2, slab, near) + entry % BRICKS
+            face = jnp.where(source > 2, slab, near) + (entry & 1)
             face = jnp.where(entry < 0, ZERO, jnp.clip(face, 0, ZERO))
             faces[b, k] = face * FACE
     owners = [owner[c // 8, c % 8] for c in range(8 * BRICKS)]
@@ -215,30 +212,43 @@
                     acc[line] = acc[line] + own[(x * 2 + b) * 8 : (x * 2 + b) * 8 + 8]
 
 
-def convolve(window, weights, total):
-    for p in range(3):
-        rows = jnp.concatenate([window[p : p + 8, t : t + 8] for t in range(3)], axis=-1)
-        part = jnp.dot(
-            rows.reshape(BRICKS * VOX, 9 * CH),
-            weights[p * 9 * CH : (p + 1) * 9 * CH],
-            preferred_element_type=jnp.float32,
-        ).reshape(OCT, BRICKS, EDGE, CH)
-        if p == 0:
-            total[...] = part
-        else:
-            total[...] += part
-
-
-def inner_kernel(step, act, weights_hbm, total, weights, window, sems):
-    copies = fetch(sems, (weights_hbm.at[step], weights))
+def convolve(window, weights, wide, total):
+    rows = jnp.concatenate([window[p : p + 8] for p in range(3)], axis=-1).reshape(BRICKS * VOX, 9 * CH)
+    taps = [
+        jnp.concatenate([weights[pl.ds((p * 3 + t) * 3 * CH, 3 * CH)] for p in range(3)], axis=0) for t in range(3)
+    ]
+    wide[...] = jnp.dot(rows, jnp.concatenate(taps, axis=1), preferred_element_type=jnp.float32)
+    line = BRICKS * EDGE
+    for x in range(EDGE):
+        for y in range(EDGE):
+            here = (x * EDGE + y) * line
+            value = wide[pl.ds(here, line), CH : 2 * CH]
+            if y > 0:
+                value = value + wide[pl.ds(here - line, line), :CH]
+            if y < 7:
+                value = value + wide[pl.ds(here + line, line), 2 * CH :]
+            total[x * EDGE + y] = value.reshape(BRICKS, EDGE, CH)
+
+
+def inner_kernel(step, act, weights_src, *rest):
+    if step == 0:
+        *tables_hbm, total, weights, faces, slots, window, wide, neighbours, kept, owner, sems = rest
+        tables = (neighbours, kept, owner)
+        copies = fetch(sems, (weights_src.at[0], weights), *zip(tables_hbm, tables))
+        for copy in copies[1:]:
+            copy.wait()
+        find_routes(*tables, faces, slots)
+    else:
+        total, window, wide = rest
+        weights = weights_src.at[step]
     blank = jnp.zeros((BRICKS * EDGE, 3 * CH), jnp.bfloat16)
     row = lax.broadcasted_iota(jnp.int32, (EDGE, CH), 0)
     for x in range(10):
-        for y in range(10):
-            if not (0 < x < 9 and 0 < y < 9):
+        for y in range(8):
+            if not 0 < x < 9:
                 window[x, y] = blank
                 continue
-            here = pl.ds(((x - 1) * 8 + y - 1) * 8, 8)
+            here = pl.ds(((x - 1) * 8 + y) * 8, 8)
             tiles = [act[b, here].astype(jnp.float32) for b in range(BRICKS)]
             shifts = (
                 [jnp.where(row > 0, pltpu.roll(t, 1, 0), 0.0) for t in tiles],
@@ -247,8 +257,9 @@
             )
             for w in range(3):
                 window[x, y, :, w * CH : (w + 1) * CH] = jnp.concatenate(shifts[w], axis=0).astype(jnp.bfloat16)
-    copies[0].wait()
-    convolve(window, weights, total)
+    if step == 0:
+        copies[0].wait()
+    convolve(window, weights, wide, total)
 
 
 def conv_kernel(
@@ -267,7 +278,7 @@
     copies = fetch(sems, (gain_hbm, gain), (shift_hbm, shift)) if step < 3 else []
     gather_halos(faces, (last, first, core, rng, slab_a, slab_b), table, field, halos)
     acc[...] = total[...].reshape(BRICKS * VOX, CH)
-    add_halos(halos, weights, acc)
+    add_halos(halos, weights.at[step] if step else weights, acc)
     if step == 3:
         packed[...] = jnp.zeros(packed.shape, packed.dtype)
     for copy in copies:
@@ -305,10 +316,17 @@
                         packed[slot] = block
 
 
-def grow_kernel(octants, up, out):
-    rows = octants[...].reshape(-1, CH)
-    grown = jnp.dot(rows, up[...], preferred_element_type=jnp.float32)
-    out[...] = grown.astype(jnp.bfloat16).reshape(out.shape)
+def grow_kernel(octants, up, out, grown, sems):
+    copies = []
+    for i in range(PARTS):
+        part = pl.ds(i * (128 // PARTS), 128 // PARTS)
+        rows = octants[part].reshape(-1, CH)
+        value = jnp.dot(rows, up[...], preferred_element_type=jnp.float32)
+        grown[part] = value.astype(jnp.bfloat16).reshape(128 // PARTS, OCT, 4 * CH)
+        copies.append(pltpu.make_async_copy(grown.at[part], out.at[part], sems.at[i]))
+        copies[-1].start()
+    for copy in copies:
+        copy.wait()
 
 
 def bf16(*shape):
@@ -342,6 +360,7 @@
     bf16(BRICKS, FACE, CH),
 ]
 LIMIT = 16 * 1024 * 1024
+PARTS = 16
 
 
 def shards(features, neighbours, keep_mask, owner, norm_gain, norm_shift, conv_weights, up_weight):
@@ -364,37 +383,44 @@
         cost_estimate=pl.CostEstimate(flops=10**7, bytes_accessed=2**22, transcendentals=2**17),
         name="start",
     )(in_hbm(features), gain, shift)
-    faces, slots = pl.pallas_call(
-        route_kernel,
-        out_shape=[jax.ShapeDtypeStruct((BRICKS, 26), jnp.int32), jax.ShapeDtypeStruct((8 * BRICKS,), jnp.int32)],
-        in_specs=[HBM, HBM, HBM, ANY],
-        out_specs=[SMEM, SMEM],
-        scratch_shapes=[
-            pltpu.SMEM((BRICKS, 26), jnp.int32),
-            pltpu.SMEM((BRICKS, 8), jnp.int32),
-            pltpu.SMEM((BRICKS, 8), jnp.int32),
-            pltpu.SemaphoreType.DMA((3,)),
-        ],
-        compiler_params=pltpu.CompilerParams(vmem_limit_bytes=LIMIT),
-        cost_estimate=pl.CostEstimate(flops=1000, bytes_accessed=4096, transcendentals=0),
-        name="route",
-    )(in_hbm(neighbours), in_hbm(keep_mask), in_hbm(owner), act)
-    all_weights = in_hbm(conv_weights.reshape(4, 27 * CH, CH))
+    all_weights = conv_weights.reshape(4, 27 * CH, CH)
     state = features
     for step in range(4):
         planes = exchange(sends)
-        total, weights = pl.pallas_call(
+        window_s = [
+            pltpu.VMEM((10, 8, BRICKS * EDGE, 3 * CH), jnp.bfloat16),
+            pltpu.VMEM((BRICKS * VOX, 3 * CH), jnp.float32),
+        ]
+        call = functools.partial(
+            pl.pallas_call,
             functools.partial(inner_kernel, step),
-            out_shape=[jax.ShapeDtypeStruct((OCT, BRICKS, EDGE, CH), jnp.float32), bf16(27 * CH, CH)],
-            in_specs=[VMEM, HBM],
-            out_specs=[VMEM, VMEM],
-            scratch_shapes=[
-                pltpu.VMEM((10, 10, BRICKS * EDGE, 3 * CH), jnp.bfloat16),
-                pltpu.SemaphoreType.DMA((1,)),
-            ],
             compiler_params=pltpu.CompilerParams(vmem_limit_bytes=LIMIT),
             cost_estimate=pl.CostEstimate(flops=2 * 10**9, bytes_accessed=2**21, transcendentals=0),
-        )(act, all_weights)
+        )
+        total_t = jax.ShapeDtypeStruct((OCT, BRICKS, EDGE, CH), jnp.float32)
+        if step == 0:
+            total, weights, faces, slots = call(
+                out_shape=[
+                    total_t,
+                    bf16(27 * CH, CH),
+                    jax.ShapeDtypeStruct((BRICKS, 26), jnp.int32),
+                    jax.ShapeDtypeStruct((8 * BRICKS,), jnp.int32),
+                ],
+                in_specs=[VMEM] + [HBM] * 4,
+                out_specs=[VMEM, VMEM, SMEM, SMEM],
+                scratch_shapes=[
+                    *window_s,
+                    pltpu.SMEM((BRICKS, 26), jnp.int32),
+                    pltpu.SMEM((BRICKS, 8), jnp.int32),
+                    pltpu.SMEM((BRICKS, 8), jnp.int32),
+                    pltpu.SemaphoreType.DMA((4,)),
+                ],
+            )(act, in_hbm(all_weights), in_hbm(neighbours), in_hbm(keep_mask), in_hbm(owner))
+        else:
+            weights = all_weights
+            (total,) = call(
+                out_shape=[total_t], in_specs=[VMEM, VMEM], out_specs=[VMEM], scratch_shapes=window_s
+            )(act, weights)
         inputs = [faces, *planes, total, weights, gain, shift]
         in_specs = [SMEM] + [VMEM] * 8 + [HBM] * 2
         if step % 2:
@@ -431,16 +457,12 @@
             if step == 1:
                 state = result[7]
     arrived = lax.all_to_all(result[0], "range", split_axis=0, concat_axis=0, tiled=True)
-    slab = 32
     return pl.pallas_call(
         grow_kernel,
-        grid=(128 // slab,),
         out_shape=bf16(128, OCT, 4 * CH),
-        in_specs=[
-            pl.BlockSpec((slab, OCT, CH), lambda i: (i, 0, 0)),
-            pl.BlockSpec((CH, 4 * CH), lambda i: (0, 0)),
-        ],
-        out_specs=pl.BlockSpec((slab, OCT, 4 * CH), lambda i: (i, 0, 0)),
+        in_specs=[VMEM, VMEM],
+        out_specs=HBM,
+        scratch_shapes=[pltpu.VMEM((128, OCT, 4 * CH), jnp.bfloat16), pltpu.SemaphoreType.DMA((PARTS,))],
         compiler_params=pltpu.CompilerParams(vmem_limit_bytes=32 * 1024 * 1024),
         name="grow",
     )(arrived, up_weight)

time: 118 us -> 116 us (0.983)
  Pallas kernels: 30.4 us -> 21.8 us
  waiting for transfers between devices: 2.42 us -> 8.77 us
    pallas_call x6 -> x5, Pallas kernels: 19.6 us -> 11 us  [the longest x3 4.4 us: shards(): call(out_shape=[total_t], in_specs=[VMEM, VMEM], out_specs=[VMEM], scratc...]
    ppermute x16, waiting for transfers between devices: 2.42 us -> 8.77 us  [swap(): return lax.ppermute(block, axis, route)]
  transfers between devices with their start and end apart: 16 -> 16, of which waited for: 3 -> 4; matrix products, arithmetic and copies ran while one was open for 0% -> 0% of each run, Pallas kernels for 13% -> 6%
where the time goes in v3:
time: 116 us; the launch traced here: 114 us
  blocking collectives  59 us (51%)
  starting transfers between devices  24.3 us (21%)
  Pallas kernels  21.8 us (19%)
  waiting for transfers between devices  8.77 us (8%)
    all_to_all x1, blocking collectives, shards(): lax.all_to_all(result[0], 'range', split_axis=0, concat_axis=0, tiled=True)  59 us
    ppermute x16, starting transfers between devices, swap(): return lax.ppermute(block, axis, route)  24.3 us
    ppermute x16, waiting for transfers between devices, swap(): return lax.ppermute(block, axis, route)  8.77 us
    pallas_call x4, Pallas kernels, shards(): pl.pallas_call(functools.partial(conv_kernel, step), out_shape=outs, in_s...  8.73 us
    pallas_call x3, Pallas kernels, shards(): call(out_shape=[total_t], in_specs=[VMEM, VMEM], out_specs=[VMEM], scratc...  4.4 us
    pallas_call x1, Pallas kernels, shards(): pl.pallas_call(grow_kernel, out_shape=bf16(128, OCT, 4 * CH), in_specs=[V...  3.69 us
    pallas_call x1, Pallas kernels, shards(): call(out_shape=[total_t, bf16(27 * CH, CH), jax.ShapeDtypeStruct((BRICKS,...  2.86 us
  transfers between devices with their start and end apart: 16, of which 4 were waited for; matrix products, arithmetic and copies ran while one was open for 0% of the time, Pallas kernels for 6%

profile of v3, /device:TPU:5, one launch (start us, length us, event | category | flops | bytes accessed | tf_op | source)
XLA Modules:
  0.0 114.2 jit_solution(8396017914668110259)
XLA Ops:
  0.0 2.1 %start.1 = (bf16[2,512,128]{2,1,0:T(8,128)(2,1)S(1)}, bf16[3,2,64,128]{3,2,1,0:T(8,128)(2,1)S(1)}, bf16[3,2,64,128]{3,2,1,0:T(8,128)(2,1)S(1)}, bf16[3,2,64,128]...) custom-call(bf16[2,512,128]{2,1,0:T(8,128)(2,1)} %rest_0_.3, ...), custom_call_target="tpu_custom_call" | custom-call | flops 10000000 | bytes 4194304 | tf_op jit(solution)/shard_map/start/pallas_call | solution.py:371
  2.1 1.0 collective-permute-start.2
  3.1 0.0 collective-permute-start.3
  3.1 2.5 %collective-permute-start = (bf16[3,2,64,128]{3,2,1,0:T(8,128)(2,1)S(1)}, bf16[3,2,64,128]{3,2,1,0:T(8,128)(2,1)S(1)}, u32[]{:S(2)}, u32[]{:S(2)}) collective-permute-start(bf16[3,2,64,128]{3,2,1,0:T(8,128)(2,1)S(1)} %get-tuple-element.42), channel_id=1, source_target_pairs={{0,1},{1,0},{2,3},{3,2},{4,5},{5,4},{6,7},{7,6},{8,9},{9,8},{10,11... | collective-permute-start | bytes 294920 | tf_op jit(solution)/shard_map/ppermute | solution.py:342
  5.6 0.0 collective-permute-start.1
  5.6 0.0 copy-start
  5.6 2.9 %shard_map.82 = (f32[64,2,8,128]{3,2,1,0:T(8,128)S(1)}, bf16[3456,128]{1,0:T(8,128)(2,1)S(1)}, s32[2,26]{1,0:T(2,128)S(1)}, s32[16]{0:T(128)S(1)}) custom-call(bf16[2,512,128]{2,1,0:T(8,128)(2,1)S(1)} %get-tuple-element.38.act, bf16[4,3456,128]{2,1,0:T(8,128)(2,1)} %bitcast.1, s32[2,26]{1,0:T(2,128)} %rest_0_.2, s32[2,8]{1,0:T(2,128)} %rest_1_.1, s32[2,8]{1,0:T(2,128)} %rest_2_.1), custom_call_target="tpu_custom_call" | custom-call | flops 2000000000 | bytes 2097152 | tf_op jit(solution)/shard_map/pallas_call | solution.py:402
  8.5 0.0 collective-permute-done.2.slab_a
  8.5 0.0 collective-permute-done.3.slab_b
  8.5 0.0 collective-permute-done.core
  8.5 1.1 collective-permute-done.1.rng
  9.7 2.2 %shard_map.83 = (bf16[2,512,128]{2,1,0:T(8,128)(2,1)S(1)}, bf16[3,2,64,128]{3,2,1,0:T(8,128)(2,1)S(1)}, bf16[3,2,64,128]{3,2,1,0:T(8,128)(2,1)S(1)}, bf16[3,2,64...) custom-call(s32[2,26]{1,0:T(2,128)S(1)} %get-tuple-element.39.faces,, ...), custom_call_target="tpu_custom_call" | custom-call | flops 500000000 | bytes 4194304 | tf_op jit(solution)/shard_map/pallas_call | solution.py:437
  11.9 0.6 collective-permute-start.6
  12.5 1.2 %collective-permute-start.7 = (bf16[2,64,128]{2,1,0:T(8,128)(2,1)S(1)}, bf16[2,64,128]{2,1,0:T(8,128)(2,1)S(1)}, u32[]{:S(2)}, u32[]{:S(2)}) collective-permute-start(bf16[2,64,128]{2,1,0:T(8,128)(2,1)S(1)} %get-tuple-element.53), channel_id=1, source_target_pairs={{0,192},{64,128},{128,64},{192,0},{1,193},{65,129},{129,65},{193,1... | collective-permute-start | bytes 98312 | tf_op jit(solution)/shard_map/ppermute | solution.py:342
  13.7 7.5 %collective-permute-start.4 = (bf16[3,2,64,128]{3,2,1,0:T(8,128)(2,1)S(1)}, bf16[3,2,64,128]{3,2,1,0:T(8,128)(2,1)S(1)}, u32[]{:S(2)}, u32[]{:S(2)}) collective-permute-start(bf16[3,2,64,128]{3,2,1,0:T(8,128)(2,1)S(1)} %get-tuple-element.50), channel_id=1, source_target_pairs={{0,1},{1,0},{2,3},{3,2},{4,5},{5,4},{6,7},{7,6},{8,9},{9,8},{10,11... | collective-permute-start | bytes 294920 | tf_op jit(solution)/shard_map/ppermute | solution.py:342
  21.2 0.0 collective-permute-start.5
  21.2 0.0 copy-done
  21.2 1.5 %shard_map.84.total = f32[64,2,8,128]{3,2,1,0:T(8,128)S(1)} custom-call(bf16[2,512,128]{2,1,0:T(8,128)(2,1)S(1)} %get-tuple-element.54.act, bf16[4,3456,128]{2,1,0:T(8,128)(2,1)S(1)} %bitcast.2), custom_call_target="tpu_custom_call" | custom-call | flops 2000000000 | bytes 2097152 | tf_op jit(solution)/shard_map/pallas_call | solution.py:421
  22.7 0.0 collective-permute-done.6.slab_a
  22.7 0.0 collective-permute-done.7.slab_b
  22.7 0.0 collective-permute-done.4.core
  22.7 2.5 %collective-permute-done.5.rng = bf16[3,2,64,128]{3,2,1,0:T(8,128)(2,1)S(1)} collective-permute-done((bf16[3,2,64,128]{3,2,1,0:T(8,128)(2,1)S(1)}, bf16[3,2,64,128]{3,2,1,0:T(8,128)(2,1)S(1)}, u32[]{:S(2)}, u32[]{:S(2)}) %collective-permute-start.5) | collective-permute-done | bytes 98336 | tf_op jit(solution)/shard_map/ppermute | solution.py:342
  25.2 0.0 copy-done.1
  25.2 2.4 %shard_map.85 = (bf16[2,512,128]{2,1,0:T(8,128)(2,1)S(1)}, bf16[3,2,64,128]{3,2,1,0:T(8,128)(2,1)S(1)}, bf16[3,2,64,128]{3,2,1,0:T(8,128)(2,1)S(1)}, bf16[3,2,64...) custom-call(s32[2,26]{1,0:T(2,128)S(1)} %get-tuple-element.39.faces,, ...), custom_call_target="tpu_custom_call" | custom-call | flops 500000000 | bytes 4194304 | tf_op jit(solution)/shard_map/pallas_call | solution.py:437
  27.6 1.0 collective-permute-start.10
  28.6 0.0 collective-permute-start.11
  28.6 3.6 %collective-permute-start.8 = (bf16[3,2,64,128]{3,2,1,0:T(8,128)(2,1)S(1)}, bf16[3,2,64,128]{3,2,1,0:T(8,128)(2,1)S(1)}, u32[]{:S(2)}, u32[]{:S(2)}) collective-permute-start(bf16[3,2,64,128]{3,2,1,0:T(8,128)(2,1)S(1)} %get-tuple-element.57), channel_id=1, source_target_pairs={{0,1},{1,0},{2,3},{3,2},{4,5},{5,4},{6,7},{7,6},{8,9},{9,8},{10,11... | collective-permute-start | bytes 294920 | tf_op jit(solution)/shard_map/ppermute | solution.py:342
  32.3 0.0 collective-permute-start.9
  32.3 1.5 %shard_map.86.total = f32[64,2,8,128]{3,2,1,0:T(8,128)S(1)} custom-call(bf16[2,512,128]{2,1,0:T(8,128)(2,1)S(1)} %get-tuple-element.61.act, bf16[4,3456,128]{2,1,0:T(8,128)(2,1)S(1)} %bitcast.4), custom_call_target="tpu_custom_call" | custom-call | flops 2000000000 | bytes 2097152 | tf_op jit(solution)/shard_map/pallas_call | solution.py:421
  33.8 0.0 collective-permute-done.10.slab_a
  33.8 0.0 collective-permute-done.11.slab_b
  33.8 0.0 collective-permute-done.8.core
  33.8 2.5 %collective-permute-done.9.rng = bf16[3,2,64,128]{3,2,1,0:T(8,128)(2,1)S(1)} collective-permute-done((bf16[3,2,64,128]{3,2,1,0:T(8,128)(2,1)S(1)}, bf16[3,2,64,128]{3,2,1,0:T(8,128)(2,1)S(1)}, u32[]{:S(2)}, u32[]{:S(2)}) %collective-permute-start.9) | collective-permute-done | bytes 98336 | tf_op jit(solution)/shard_map/ppermute | solution.py:342
  36.3 2.2 %shard_map.87 = (bf16[2,512,128]{2,1,0:T(8,128)(2,1)S(1)}, bf16[3,2,64,128]{3,2,1,0:T(8,128)(2,1)S(1)}, bf16[3,2,64,128]{3,2,1,0:T(8,128)(2,1)S(1)}, bf16[3,2,64...) custom-call(s32[2,26]{1,0:T(2,128)S(1)} %get-tuple-element.39.faces,, ...), custom_call_target="tpu_custom_call" | custom-call | flops 500000000 | bytes 4194304 | tf_op jit(solution)/shard_map/pallas_call | solution.py:437
  38.6 1.7 %collective-permute-start.14 = (bf16[2,64,128]{2,1,0:T(8,128)(2,1)S(1)}, bf16[2,64,128]{2,1,0:T(8,128)(2,1)S(1)}, u32[]{:S(2)}, u32[]{:S(2)}) collective-permute-start(bf16[2,64,128]{2,1,0:T(8,128)(2,1)S(1)} %get-tuple-element.66), channel_id=1, source_target_pairs={{0,64},{64,0},{128,192},{192,128},{1,65},{65,1},{129,193},{193,129... | collective-permute-start | bytes 98312 | tf_op jit(solution)/shard_map/ppermute | solution.py:342
  40.3 1.2 %collective-permute-start.15 = (bf16[2,64,128]{2,1,0:T(8,128)(2,1)S(1)}, bf16[2,64,128]{2,1,0:T(8,128)(2,1)S(1)}, u32[]{:S(2)}, u32[]{:S(2)}) collective-permute-start(bf16[2,64,128]{2,1,0:T(8,128)(2,1)S(1)} %get-tuple-element.67), channel_id=1, source_target_pairs={{0,192},{64,128},{128,64},{192,0},{1,193},{65,129},{129,65},{193,1... | collective-permute-start | bytes 98312 | tf_op jit(solution)/shard_map/ppermute | solution.py:342
  41.5 3.9 %collective-permute-start.12 = (bf16[3,2,64,128]{3,2,1,0:T(8,128)(2,1)S(1)}, bf16[3,2,64,128]{3,2,1,0:T(8,128)(2,1)S(1)}, u32[]{:S(2)}, u32[]{:S(2)}) collective-permute-start(bf16[3,2,64,128]{3,2,1,0:T(8,128)(2,1)S(1)} %get-tuple-element.64), channel_id=1, source_target_pairs={{0,1},{1,0},{2,3},{3,2},{4,5},{5,4},{6,7},{7,6},{8,9},{9,8},{10,11... | collective-permute-start | bytes 294920 | tf_op jit(solution)/shard_map/ppermute | solution.py:342
  45.4 0.0 collective-permute-start.13
  45.4 1.5 %shard_map.88.total = f32[64,2,8,128]{3,2,1,0:T(8,128)S(1)} custom-call(bf16[2,512,128]{2,1,0:T(8,128)(2,1)S(1)} %get-tuple-element.68.act, bf16[4,3456,128]{2,1,0:T(8,128)(2,1)S(1)} %bitcast.6), custom_call_target="tpu_custom_call" | custom-call | flops 2000000000 | bytes 2097152 | tf_op jit(solution)/shard_map/pallas_call | solution.py:421
  46.9 0.0 collective-permute-done.14.slab_a
  46.9 0.0 collective-permute-done.15.slab_b
  46.9 0.0 collective-permute-done.12.core
  46.9 2.5 %collective-permute-done.13.rng = bf16[3,2,64,128]{3,2,1,0:T(8,128)(2,1)S(1)} collective-permute-done((bf16[3,2,64,128]{3,2,1,0:T(8,128)(2,1)S(1)}, bf16[3,2,64,128]{3,2,1,0:T(8,128)(2,1)S(1)}, u32[]{:S(2)}, u32[]{:S(2)}) %collective-permute-start.13) | collective-permute-done | bytes 98336 | tf_op jit(solution)/shard_map/ppermute | solution.py:342
  49.4 1.9 %shard_map.89 = bf16[128,64,128]{2,1,0:T(8,128)(2,1)S(1)} custom-call(s32[2,26]{1,0:T(2,128)S(1)} %get-tuple-element.39.faces, bf16[3,2,64,128]{3,2,1,0:T(8,128)(2,1)S(1)} %get-tuple-element.62.last, bf16[3,2,64,128]{3,2,1,0:T(8,128)(2,1)S(1)} %get-tuple-element.63.first, bf16[3,2,64,128]{3,2,1,0:T(8,128)(2,1)S(1)} %collective-permute-done.12.core, ...), custom_call_target="tpu_custom_call" | custom-call | flops 500000000 | bytes 4194304 | tf_op jit(solution)/shard_map/pallas_call | solution.py:437
  51.3 0.0 copy-start.2
  51.3 59.0 %all_to_all.5.octants = bf16[128,64,128]{2,1,0:T(8,128)(2,1)S(1)} all-to-all(bf16[128,64,128]{2,1,0:T(8,128)(2,1)S(1)} %shard_map.89), channel_id=1, replica_groups=mesh['slab'=4,'range'=64] {'range'}, dimensions={0} | all-to-all | bytes 4194304 | tf_op jit(solution)/shard_map/all_to_all | solution.py:459
  110.4 0.0 copy-done.2
  110.4 3.7 %grow.1 = bf16[128,64,512]{2,1,0:T(8,128)(2,1)} custom-call(bf16[128,64,128]{2,1,0:T(8,128)(2,1)S(1)} %all_to_all.5.octants, bf16[128,512]{1,0:T(8,128)(2,1)S(1)} %copy-done.2), custom_call_target="tpu_custom_call" | custom-call | tf_op jit(solution)/shard_map/grow/pallas_call | solution.py:460
  (1 shorter events, 0.0 us)
Async XLA Ops:
  2.1 6.4 %collective-permute-start.2 = (bf16[2,64,128]{2,1,0:T(8,128)(2,1)S(1)}, bf16[2,64,128]{2,1,0:T(8,128)(2,1)S(1)}, u32[]{:S(2)}, u32[]{:S(2)}) collective-permute-start(bf16[2,64,128]{2,1,0:T(8,128)(2,1)S(1)} %get-tuple-element.44), channel_id=1, source_target_pairs={{0,64},{64,0},{128,192},{192,128},{1,65},{65,1},{129,193},{193,129... | collective-permute-start | bytes 98312 | tf_op jit(solution)/shard_map/ppermute | solution.py:342
  3.1 5.4 %collective-permute-start.3 = (bf16[2,64,128]{2,1,0:T(8,128)(2,1)S(1)}, bf16[2,64,128]{2,1,0:T(8,128)(2,1)S(1)}, u32[]{:S(2)}, u32[]{:S(2)}) collective-permute-start(bf16[2,64,128]{2,1,0:T(8,128)(2,1)S(1)} %get-tuple-element.45), channel_id=1, source_target_pairs={{0,192},{64,128},{128,64},{192,0},{1,193},{65,129},{129,65},{193,1... | collective-permute-start | bytes 98312 | tf_op jit(solution)/shard_map/ppermute | solution.py:342
  3.1 5.4 %collective-permute-start = (bf16[3,2,64,128]{3,2,1,0:T(8,128)(2,1)S(1)}, bf16[3,2,64,128]{3,2,1,0:T(8,128)(2,1)S(1)}, u32[]{:S(2)}, u32[]{:S(2)}) collective-permute-start(bf16[3,2,64,128]{3,2,1,0:T(8,128)(2,1)S(1)} %get-tuple-element.42), channel_id=1, source_target_pairs={{0,1},{1,0},{2,3},{3,2},{4,5},{5,4},{6,7},{7,6},{8,9},{9,8},{10,11... | collective-permute-start | bytes 294920 | tf_op jit(solution)/shard_map/ppermute | solution.py:342
  5.6 4.0 %collective-permute-start.1 = (bf16[3,2,64,128]{3,2,1,0:T(8,128)(2,1)S(1)}, bf16[3,2,64,128]{3,2,1,0:T(8,128)(2,1)S(1)}, u32[]{:S(2)}, u32[]{:S(2)}) collective-permute-start(bf16[3,2,64,128]{3,2,1,0:T(8,128)(2,1)S(1)} %get-tuple-element.43), channel_id=1, source_target_pairs={{0,63},{1,2},{2,1},{3,4},{4,3},{5,6},{6,5},{7,8},{8,7},{9,10},{10,... | collective-permute-start | bytes 294920 | tf_op jit(solution)/shard_map/ppermute | solution.py:342
  5.6 15.6 %copy-start = (bf16[4,27,128,128]{3,2,1,0:T(8,128)(2,1)S(1)}, bf16[4,27,128,128]{3,2,1,0:T(8,128)(2,1)}, u32[]{:S(2)}) copy-start(bf16[4,27,128,128]{3,2,1,0:T(8,128)(2,1)} %param.14) | copy-start | bytes 10616836
  11.9 10.8 %collective-permute-start.6 = (bf16[2,64,128]{2,1,0:T(8,128)(2,1)S(1)}, bf16[2,64,128]{2,1,0:T(8,128)(2,1)S(1)}, u32[]{:S(2)}, u32[]{:S(2)}) collective-permute-start(bf16[2,64,128]{2,1,0:T(8,128)(2,1)S(1)} %get-tuple-element.52), channel_id=1, source_target_pairs={{0,64},{64,0},{128,192},{192,128},{1,65},{65,1},{129,193},{193,129... | collective-permute-start | bytes 98312 | tf_op jit(solution)/shard_map/ppermute | solution.py:342
  12.5 10.2 %collective-permute-start.7 = (bf16[2,64,128]{2,1,0:T(8,128)(2,1)S(1)}, bf16[2,64,128]{2,1,0:T(8,128)(2,1)S(1)}, u32[]{:S(2)}, u32[]{:S(2)}) collective-permute-start(bf16[2,64,128]{2,1,0:T(8,128)(2,1)S(1)} %get-tuple-element.53), channel_id=1, source_target_pairs={{0,192},{64,128},{128,64},{192,0},{1,193},{65,129},{129,65},{193,1... | collective-permute-start | bytes 98312 | tf_op jit(solution)/shard_map/ppermute | solution.py:342
  13.7 9.0 %collective-permute-start.4 = (bf16[3,2,64,128]{3,2,1,0:T(8,128)(2,1)S(1)}, bf16[3,2,64,128]{3,2,1,0:T(8,128)(2,1)S(1)}, u32[]{:S(2)}, u32[]{:S(2)}) collective-permute-start(bf16[3,2,64,128]{3,2,1,0:T(8,128)(2,1)S(1)} %get-tuple-element.50), channel_id=1, source_target_pairs={{0,1},{1,0},{2,3},{3,2},{4,5},{5,4},{6,7},{7,6},{8,9},{9,8},{10,11... | collective-permute-start | bytes 294920 | tf_op jit(solution)/shard_map/ppermute | solution.py:342
  21.2 4.0 %collective-permute-start.5 = (bf16[3,2,64,128]{3,2,1,0:T(8,128)(2,1)S(1)}, bf16[3,2,64,128]{3,2,1,0:T(8,128)(2,1)S(1)}, u32[]{:S(2)}, u32[]{:S(2)}) collective-permute-start(bf16[3,2,64,128]{3,2,1,0:T(8,128)(2,1)S(1)} %get-tuple-element.51), channel_id=1, source_target_pairs={{0,63},{1,2},{2,1},{3,4},{4,3},{5,6},{6,5},{7,8},{8,7},{9,10},{10,... | collective-permute-start | bytes 294920 | tf_op jit(solution)/shard_map/ppermute | solution.py:342
  21.2 4.0 %copy-start.1 = (bf16[2,512,128]{2,1,0:T(8,128)(2,1)S(1)}, bf16[2,512,128]{2,1,0:T(8,128)(2,1)}, u32[]{:S(2)}) copy-start(bf16[2,512,128]{2,1,0:T(8,128)(2,1)} %rest_0_.3) | copy-start | bytes 786436
  27.6 6.1 %collective-permute-start.10 = (bf16[2,64,128]{2,1,0:T(8,128)(2,1)S(1)}, bf16[2,64,128]{2,1,0:T(8,128)(2,1)S(1)}, u32[]{:S(2)}, u32[]{:S(2)}) collective-permute-start(bf16[2,64,128]{2,1,0:T(8,128)(2,1)S(1)} %get-tuple-element.59), channel_id=1, source_target_pairs={{0,64},{64,0},{128,192},{192,128},{1,65},{65,1},{129,193},{193,129... | collective-permute-start | bytes 98312 | tf_op jit(solution)/shard_map/ppermute | solution.py:342
  28.6 5.1 %collective-permute-start.11 = (bf16[2,64,128]{2,1,0:T(8,128)(2,1)S(1)}, bf16[2,64,128]{2,1,0:T(8,128)(2,1)S(1)}, u32[]{:S(2)}, u32[]{:S(2)}) collective-permute-start(bf16[2,64,128]{2,1,0:T(8,128)(2,1)S(1)} %get-tuple-element.60), channel_id=1, source_target_pairs={{0,192},{64,128},{128,64},{192,0},{1,193},{65,129},{129,65},{193,1... | collective-permute-start | bytes 98312 | tf_op jit(solution)/shard_map/ppermute | solution.py:342
  28.6 5.2 %collective-permute-start.8 = (bf16[3,2,64,128]{3,2,1,0:T(8,128)(2,1)S(1)}, bf16[3,2,64,128]{3,2,1,0:T(8,128)(2,1)S(1)}, u32[]{:S(2)}, u32[]{:S(2)}) collective-permute-start(bf16[3,2,64,128]{3,2,1,0:T(8,128)(2,1)S(1)} %get-tuple-element.57), channel_id=1, source_target_pairs={{0,1},{1,0},{2,3},{3,2},{4,5},{5,4},{6,7},{7,6},{8,9},{9,8},{10,11... | collective-permute-start | bytes 294920 | tf_op jit(solution)/shard_map/ppermute | solution.py:342
  32.3 4.0 %collective-permute-start.9 = (bf16[3,2,64,128]{3,2,1,0:T(8,128)(2,1)S(1)}, bf16[3,2,64,128]{3,2,1,0:T(8,128)(2,1)S(1)}, u32[]{:S(2)}, u32[]{:S(2)}) collective-permute-start(bf16[3,2,64,128]{3,2,1,0:T(8,128)(2,1)S(1)} %get-tuple-element.58), channel_id=1, source_target_pairs={{0,63},{1,2},{2,1},{3,4},{4,3},{5,6},{6,5},{7,8},{8,7},{9,10},{10,... | collective-permute-start | bytes 294920 | tf_op jit(solution)/shard_map/ppermute | solution.py:342
  38.6 8.3 %collective-permute-start.14 = (bf16[2,64,128]{2,1,0:T(8,128)(2,1)S(1)}, bf16[2,64,128]{2,1,0:T(8,128)(2,1)S(1)}, u32[]{:S(2)}, u32[]{:S(2)}) collective-permute-start(bf16[2,64,128]{2,1,0:T(8,128)(2,1)S(1)} %get-tuple-element.66), channel_id=1, source_target_pairs={{0,64},{64,0},{128,192},{192,128},{1,65},{65,1},{129,193},{193,129... | collective-permute-start | bytes 98312 | tf_op jit(solution)/shard_map/ppermute | solution.py:342
  40.3 6.6 %collective-permute-start.15 = (bf16[2,64,128]{2,1,0:T(8,128)(2,1)S(1)}, bf16[2,64,128]{2,1,0:T(8,128)(2,1)S(1)}, u32[]{:S(2)}, u32[]{:S(2)}) collective-permute-start(bf16[2,64,128]{2,1,0:T(8,128)(2,1)S(1)} %get-tuple-element.67), channel_id=1, source_target_pairs={{0,192},{64,128},{128,64},{192,0},{1,193},{65,129},{129,65},{193,1... | collective-permute-start | bytes 98312 | tf_op jit(solution)/shard_map/ppermute | solution.py:342
  41.5 5.4 %collective-permute-start.12 = (bf16[3,2,64,128]{3,2,1,0:T(8,128)(2,1)S(1)}, bf16[3,2,64,128]{3,2,1,0:T(8,128)(2,1)S(1)}, u32[]{:S(2)}, u32[]{:S(2)}) collective-permute-start(bf16[3,2,64,128]{3,2,1,0:T(8,128)(2,1)S(1)} %get-tuple-element.64), channel_id=1, source_target_pairs={{0,1},{1,0},{2,3},{3,2},{4,5},{5,4},{6,7},{7,6},{8,9},{9,8},{10,11... | collective-permute-start | bytes 294920 | tf_op jit(solution)/shard_map/ppermute | solution.py:342
  45.4 4.0 %collective-permute-start.13 = (bf16[3,2,64,128]{3,2,1,0:T(8,128)(2,1)S(1)}, bf16[3,2,64,128]{3,2,1,0:T(8,128)(2,1)S(1)}, u32[]{:S(2)}, u32[]{:S(2)}) collective-permute-start(bf16[3,2,64,128]{3,2,1,0:T(8,128)(2,1)S(1)} %get-tuple-element.65), channel_id=1, source_target_pairs={{0,63},{1,2},{2,1},{3,4},{4,3},{5,6},{6,5},{7,8},{8,7},{9,10},{10,... | collective-permute-start | bytes 294920 | tf_op jit(solution)/shard_map/ppermute | solution.py:342
  51.3 59.0 %copy-start.2 = (bf16[128,512]{1,0:T(8,128)(2,1)S(1)}, bf16[128,512]{1,0:T(8,128)(2,1)}, u32[]{:S(2)}) copy-start(bf16[128,512]{1,0:T(8,128)(2,1)} %up.1) | copy-start | bytes 393220

commit v4 on v3

--- a/solution.py
+++ b/solution.py
@@ -334,12 +334,18 @@
 
 
 def swap(block, axis, odd):
-    count = lax.axis_size(axis)
+    slabs, ranges = lax.axis_size("slab"), lax.axis_size("range")
     route = []
-    for i in range(count):
-        j = (i ^ 1) if not odd else (i + 1 if i % 2 else i - 1)
-        route.append((i, j % count))
-    return lax.ppermute(block, axis, route)
+    for s in range(slabs):
+        for r in range(ranges):
+            step = 1 if (s if axis == "slab" else r) % 2 == odd else -1
+            to = [s + step, r] if axis == "slab" else [s, r + step]
+            if not 0 <= to[0] < slabs:
+                to = [s, r ^ 1]
+            if not 0 <= to[1] < ranges:
+                to = [s ^ 1, r]
+            route.append((s * ranges + r, to[0] * ranges + to[1]))
+    return lax.ppermute(block, ("slab", "range"), route)
 
 
 def exchange(sends):

time: 116 us -> 109 us (0.940)
  starting transfers between devices: 24.3 us -> 11.7 us
  blocking collectives: 59 us -> 65.9 us
    ppermute x16, starting transfers between devices: 24.3 us -> 11.7 us  [swap(): return lax.ppermute(block, ('slab', 'range'), route)]
    all_to_all x1, blocking collectives: 59 us -> 65.9 us  [shards(): lax.all_to_all(result[0], 'range', split_axis=0, concat_axis=0, tiled=True)]
  transfers between devices with their start and end apart: 16 -> 16, of which waited for: 4 -> 4; matrix products, arithmetic and copies ran while one was open for 0% -> 0% of each run, Pallas kernels for 6% -> 7%
where the time goes in v4:
time: 109 us; the launch traced here: 107 us
  blocking collectives  65.9 us (60%)
  Pallas kernels  21.8 us (20%)
  starting transfers between devices  11.7 us (11%)
  waiting for transfers between devices  7.65 us (7%)
    all_to_all x1, blocking collectives, shards(): lax.all_to_all(result[0], 'range', split_axis=0, concat_axis=0, tiled=True)  65.9 us
    ppermute x16, starting transfers between devices, swap(): return lax.ppermute(block, ('slab', 'range'), route)  11.7 us
    pallas_call x4, Pallas kernels, shards(): pl.pallas_call(functools.partial(conv_kernel, step), out_shape=outs, in_s...  8.73 us
    ppermute x16, waiting for transfers between devices, swap(): return lax.ppermute(block, ('slab', 'range'), route)  7.65 us
    pallas_call x3, Pallas kernels, shards(): call(out_shape=[total_t], in_specs=[VMEM, VMEM], out_specs=[VMEM], scratc...  4.4 us
    pallas_call x1, Pallas kernels, shards(): pl.pallas_call(grow_kernel, out_shape=bf16(128, OCT, 4 * CH), in_specs=[V...  3.69 us
    pallas_call x1, Pallas kernels, shards(): call(out_shape=[total_t, bf16(27 * CH, CH), jax.ShapeDtypeStruct((BRICKS,...  2.86 us
  transfers between devices with their start and end apart: 16, of which 4 were waited for; matrix products, arithmetic and copies ran while one was open for 0% of the time, Pallas kernels for 7%

profile of v4, /device:TPU:5, one launch (start us, length us, event | category | flops | bytes accessed | tf_op | source)
XLA Modules:
  0.0 107.5 jit_solution(7539278797896820725)
XLA Ops:
  0.0 2.1 %start.1 = (bf16[2,512,128]{2,1,0:T(8,128)(2,1)S(1)}, bf16[3,2,64,128]{3,2,1,0:T(8,128)(2,1)S(1)}, bf16[3,2,64,128]{3,2,1,0:T(8,128)(2,1)S(1)}, bf16[3,2,64,128]...) custom-call(bf16[2,512,128]{2,1,0:T(8,128)(2,1)} %rest_0_.3, ...), custom_call_target="tpu_custom_call" | custom-call | flops 10000000 | bytes 4194304 | tf_op jit(solution)/shard_map/start/pallas_call | solution.py:377
  2.1 1.0 collective-permute-start.2
  3.1 0.0 collective-permute-start.3
  3.1 2.5 %collective-permute-start = (bf16[3,2,64,128]{3,2,1,0:T(8,128)(2,1)S(1)}, bf16[3,2,64,128]{3,2,1,0:T(8,128)(2,1)S(1)}, u32[]{:S(2)}, u32[]{:S(2)}) collective-permute-start(bf16[3,2,64,128]{3,2,1,0:T(8,128)(2,1)S(1)} %get-tuple-element.42), channel_id=1, source_target_pairs={{0,1},{1,0},{2,3},{3,2},{4,5},{5,4},{6,7},{7,6},{8,9},{9,8},{10,11... | collective-permute-start | bytes 294920 | tf_op jit(solution)/shard_map/ppermute | solution.py:348
  5.6 0.0 collective-permute-start.1
  5.6 0.0 copy-start
  5.6 2.9 %shard_map.82 = (f32[64,2,8,128]{3,2,1,0:T(8,128)S(1)}, bf16[3456,128]{1,0:T(8,128)(2,1)S(1)}, s32[2,26]{1,0:T(2,128)S(1)}, s32[16]{0:T(128)S(1)}) custom-call(bf16[2,512,128]{2,1,0:T(8,128)(2,1)S(1)} %get-tuple-element.38.act, bf16[4,3456,128]{2,1,0:T(8,128)(2,1)} %bitcast.1, s32[2,26]{1,0:T(2,128)} %rest_0_.2, s32[2,8]{1,0:T(2,128)} %rest_1_.1, s32[2,8]{1,0:T(2,128)} %rest_2_.1), custom_call_target="tpu_custom_call" | custom-call | flops 2000000000 | bytes 2097152 | tf_op jit(solution)/shard_map/pallas_call | solution.py:408
  8.5 0.0 collective-permute-done.2.slab_a
  8.5 0.0 collective-permute-done.3.slab_b
  8.5 0.0 collective-permute-done.core
  8.5 1.3 %collective-permute-done.1.rng = bf16[3,2,64,128]{3,2,1,0:T(8,128)(2,1)S(1)} collective-permute-done((bf16[3,2,64,128]{3,2,1,0:T(8,128)(2,1)S(1)}, bf16[3,2,64,128]{3,2,1,0:T(8,128)(2,1)S(1)}, u32[]{:S(2)}, u32[]{:S(2)}) %collective-permute-start.1) | collective-permute-done | bytes 98336 | tf_op jit(solution)/shard_map/ppermute | solution.py:348
  9.9 2.2 %shard_map.83 = (bf16[2,512,128]{2,1,0:T(8,128)(2,1)S(1)}, bf16[3,2,64,128]{3,2,1,0:T(8,128)(2,1)S(1)}, bf16[3,2,64,128]{3,2,1,0:T(8,128)(2,1)S(1)}, bf16[3,2,64...) custom-call(s32[2,26]{1,0:T(2,128)S(1)} %get-tuple-element.39.faces,, ...), custom_call_target="tpu_custom_call" | custom-call | flops 500000000 | bytes 4194304 | tf_op jit(solution)/shard_map/pallas_call | solution.py:443
  12.1 0.1 collective-permute-start.6
  12.2 0.5 collective-permute-start.7
  12.7 0.7 collective-permute-start.4
  13.4 1.4 %collective-permute-start.5 = (bf16[3,2,64,128]{3,2,1,0:T(8,128)(2,1)S(1)}, bf16[3,2,64,128]{3,2,1,0:T(8,128)(2,1)S(1)}, u32[]{:S(2)}, u32[]{:S(2)}) collective-permute-start(bf16[3,2,64,128]{3,2,1,0:T(8,128)(2,1)S(1)} %get-tuple-element.51), channel_id=1, source_target_pairs={{0,64},{1,2},{2,1},{3,4},{4,3},{5,6},{6,5},{7,8},{8,7},{9,10},{10,... | collective-permute-start | bytes 294920 | tf_op jit(solution)/shard_map/ppermute | solution.py:348
  14.7 0.0 copy-done
  14.7 1.5 %shard_map.84.total = f32[64,2,8,128]{3,2,1,0:T(8,128)S(1)} custom-call(bf16[2,512,128]{2,1,0:T(8,128)(2,1)S(1)} %get-tuple-element.54.act, bf16[4,3456,128]{2,1,0:T(8,128)(2,1)S(1)} %bitcast.2), custom_call_target="tpu_custom_call" | custom-call | flops 2000000000 | bytes 2097152 | tf_op jit(solution)/shard_map/pallas_call | solution.py:427
  16.2 0.0 collective-permute-done.6.slab_a
  16.2 0.0 collective-permute-done.7.slab_b
  16.2 0.0 collective-permute-done.4.core
  16.2 1.4 %collective-permute-done.5.rng = bf16[3,2,64,128]{3,2,1,0:T(8,128)(2,1)S(1)} collective-permute-done((bf16[3,2,64,128]{3,2,1,0:T(8,128)(2,1)S(1)}, bf16[3,2,64,128]{3,2,1,0:T(8,128)(2,1)S(1)}, u32[]{:S(2)}, u32[]{:S(2)}) %collective-permute-start.5) | collective-permute-done | bytes 98336 | tf_op jit(solution)/shard_map/ppermute | solution.py:348
  17.6 0.0 copy-done.1
  17.6 2.4 %shard_map.85 = (bf16[2,512,128]{2,1,0:T(8,128)(2,1)S(1)}, bf16[3,2,64,128]{3,2,1,0:T(8,128)(2,1)S(1)}, bf16[3,2,64,128]{3,2,1,0:T(8,128)(2,1)S(1)}, bf16[3,2,64...) custom-call(s32[2,26]{1,0:T(2,128)S(1)} %get-tuple-element.39.faces,, ...), custom_call_target="tpu_custom_call" | custom-call | flops 500000000 | bytes 4194304 | tf_op jit(solution)/shard_map/pallas_call | solution.py:443
  20.0 1.2 %collective-permute-start.10 = (bf16[2,64,128]{2,1,0:T(8,128)(2,1)S(1)}, bf16[2,64,128]{2,1,0:T(8,128)(2,1)S(1)}, u32[]{:S(2)}, u32[]{:S(2)}) collective-permute-start(bf16[2,64,128]{2,1,0:T(8,128)(2,1)S(1)} %get-tuple-element.59), channel_id=1, source_target_pairs={{0,64},{1,65},{2,66},{3,67},{4,68},{5,69},{6,70},{7,71},{8,72},{9,... | collective-permute-start | bytes 98312 | tf_op jit(solution)/shard_map/ppermute | solution.py:348
  21.2 0.3 collective-permute-start.11
  21.5 1.2 %collective-permute-start.8 = (bf16[3,2,64,128]{3,2,1,0:T(8,128)(2,1)S(1)}, bf16[3,2,64,128]{3,2,1,0:T(8,128)(2,1)S(1)}, u32[]{:S(2)}, u32[]{:S(2)}) collective-permute-start(bf16[3,2,64,128]{3,2,1,0:T(8,128)(2,1)S(1)} %get-tuple-element.57), channel_id=1, source_target_pairs={{0,1},{1,0},{2,3},{3,2},{4,5},{5,4},{6,7},{7,6},{8,9},{9,8},{10,11... | collective-permute-start | bytes 294920 | tf_op jit(solution)/shard_map/ppermute | solution.py:348
  22.7 0.5 collective-permute-start.9
  23.2 1.5 %shard_map.86.total = f32[64,2,8,128]{3,2,1,0:T(8,128)S(1)} custom-call(bf16[2,512,128]{2,1,0:T(8,128)(2,1)S(1)} %get-tuple-element.61.act, bf16[4,3456,128]{2,1,0:T(8,128)(2,1)S(1)} %bitcast.4), custom_call_target="tpu_custom_call" | custom-call | flops 2000000000 | bytes 2097152 | tf_op jit(solution)/shard_map/pallas_call | solution.py:427
  24.6 0.0 collective-permute-done.10.slab_a
  24.7 0.0 collective-permute-done.11.slab_b
  24.7 0.0 collective-permute-done.8.core
  24.7 2.2 %collective-permute-done.9.rng = bf16[3,2,64,128]{3,2,1,0:T(8,128)(2,1)S(1)} collective-permute-done((bf16[3,2,64,128]{3,2,1,0:T(8,128)(2,1)S(1)}, bf16[3,2,64,128]{3,2,1,0:T(8,128)(2,1)S(1)}, u32[]{:S(2)}, u32[]{:S(2)}) %collective-permute-start.9) | collective-permute-done | bytes 98336 | tf_op jit(solution)/shard_map/ppermute | solution.py:348
  26.9 2.2 %shard_map.87 = (bf16[2,512,128]{2,1,0:T(8,128)(2,1)S(1)}, bf16[3,2,64,128]{3,2,1,0:T(8,128)(2,1)S(1)}, bf16[3,2,64,128]{3,2,1,0:T(8,128)(2,1)S(1)}, bf16[3,2,64...) custom-call(s32[2,26]{1,0:T(2,128)S(1)} %get-tuple-element.39.faces,, ...), custom_call_target="tpu_custom_call" | custom-call | flops 500000000 | bytes 4194304 | tf_op jit(solution)/shard_map/pallas_call | solution.py:443
  29.1 0.1 collective-permute-start.14
  29.2 1.4 %collective-permute-start.15 = (bf16[2,64,128]{2,1,0:T(8,128)(2,1)S(1)}, bf16[2,64,128]{2,1,0:T(8,128)(2,1)S(1)}, u32[]{:S(2)}, u32[]{:S(2)}) collective-permute-start(bf16[2,64,128]{2,1,0:T(8,128)(2,1)S(1)} %get-tuple-element.67), channel_id=1, source_target_pairs={{0,1},{1,0},{2,3},{3,2},{4,5},{5,4},{6,7},{7,6},{8,9},{9,8},{10,11... | collective-permute-start | bytes 98312 | tf_op jit(solution)/shard_map/ppermute | solution.py:348
  30.6 0.9 collective-permute-start.12
  31.5 0.0 collective-permute-start.13
  31.5 1.5 %shard_map.88.total = f32[64,2,8,128]{3,2,1,0:T(8,128)S(1)} custom-call(bf16[2,512,128]{2,1,0:T(8,128)(2,1)S(1)} %get-tuple-element.68.act, bf16[4,3456,128]{2,1,0:T(8,128)(2,1)S(1)} %bitcast.6), custom_call_target="tpu_custom_call" | custom-call | flops 2000000000 | bytes 2097152 | tf_op jit(solution)/shard_map/pallas_call | solution.py:427
  33.0 0.0 collective-permute-done.14.slab_a
  33.0 0.0 collective-permute-done.15.slab_b
  33.0 0.0 collective-permute-done.12.core
  33.0 2.7 %collective-permute-done.13.rng = bf16[3,2,64,128]{3,2,1,0:T(8,128)(2,1)S(1)} collective-permute-done((bf16[3,2,64,128]{3,2,1,0:T(8,128)(2,1)S(1)}, bf16[3,2,64,128]{3,2,1,0:T(8,128)(2,1)S(1)}, u32[]{:S(2)}, u32[]{:S(2)}) %collective-permute-start.13) | collective-permute-done | bytes 98336 | tf_op jit(solution)/shard_map/ppermute | solution.py:348
  35.8 1.9 %shard_map.89 = bf16[128,64,128]{2,1,0:T(8,128)(2,1)S(1)} custom-call(s32[2,26]{1,0:T(2,128)S(1)} %get-tuple-element.39.faces, bf16[3,2,64,128]{3,2,1,0:T(8,128)(2,1)S(1)} %get-tuple-element.62.last, bf16[3,2,64,128]{3,2,1,0:T(8,128)(2,1)S(1)} %get-tuple-element.63.first, bf16[3,2,64,128]{3,2,1,0:T(8,128)(2,1)S(1)} %collective-permute-done.12.core, ...), custom_call_target="tpu_custom_call" | custom-call | flops 500000000 | bytes 4194304 | tf_op jit(solution)/shard_map/pallas_call | solution.py:443
  37.6 0.0 copy-start.2
  37.7 65.9 %all_to_all.5.octants = bf16[128,64,128]{2,1,0:T(8,128)(2,1)S(1)} all-to-all(bf16[128,64,128]{2,1,0:T(8,128)(2,1)S(1)} %shard_map.89), channel_id=1, replica_groups=mesh['slab'=4,'range'=64] {'range'}, dimensions={0} | all-to-all | bytes 4194304 | tf_op jit(solution)/shard_map/all_to_all | solution.py:465
  103.6 0.0 copy-done.2
  103.6 3.7 %grow.1 = bf16[128,64,512]{2,1,0:T(8,128)(2,1)} custom-call(bf16[128,64,128]{2,1,0:T(8,128)(2,1)S(1)} %all_to_all.5.octants, bf16[128,512]{1,0:T(8,128)(2,1)S(1)} %copy-done.2), custom_call_target="tpu_custom_call" | custom-call | tf_op jit(solution)/shard_map/grow/pallas_call | solution.py:466
  (1 shorter events, 0.0 us)
Async XLA Ops:
  2.1 6.4 %collective-permute-start.2 = (bf16[2,64,128]{2,1,0:T(8,128)(2,1)S(1)}, bf16[2,64,128]{2,1,0:T(8,128)(2,1)S(1)}, u32[]{:S(2)}, u32[]{:S(2)}) collective-permute-start(bf16[2,64,128]{2,1,0:T(8,128)(2,1)S(1)} %get-tuple-element.44), channel_id=1, source_target_pairs={{0,64},{1,65},{2,66},{3,67},{4,68},{5,69},{6,70},{7,71},{8,72},{9,... | collective-permute-start | bytes 98312 | tf_op jit(solution)/shard_map/ppermute | solution.py:348
  3.1 5.4 %collective-permute-start.3 = (bf16[2,64,128]{2,1,0:T(8,128)(2,1)S(1)}, bf16[2,64,128]{2,1,0:T(8,128)(2,1)S(1)}, u32[]{:S(2)}, u32[]{:S(2)}) collective-permute-start(bf16[2,64,128]{2,1,0:T(8,128)(2,1)S(1)} %get-tuple-element.45), channel_id=1, source_target_pairs={{0,1},{1,0},{2,3},{3,2},{4,5},{5,4},{6,7},{7,6},{8,9},{9,8},{10,11... | collective-permute-start | bytes 98312 | tf_op jit(solution)/shard_map/ppermute | solution.py:348
  3.1 5.4 %collective-permute-start = (bf16[3,2,64,128]{3,2,1,0:T(8,128)(2,1)S(1)}, bf16[3,2,64,128]{3,2,1,0:T(8,128)(2,1)S(1)}, u32[]{:S(2)}, u32[]{:S(2)}) collective-permute-start(bf16[3,2,64,128]{3,2,1,0:T(8,128)(2,1)S(1)} %get-tuple-element.42), channel_id=1, source_target_pairs={{0,1},{1,0},{2,3},{3,2},{4,5},{5,4},{6,7},{7,6},{8,9},{9,8},{10,11... | collective-permute-start | bytes 294920 | tf_op jit(solution)/shard_map/ppermute | solution.py:348
  5.6 4.2 %collective-permute-start.1 = (bf16[3,2,64,128]{3,2,1,0:T(8,128)(2,1)S(1)}, bf16[3,2,64,128]{3,2,1,0:T(8,128)(2,1)S(1)}, u32[]{:S(2)}, u32[]{:S(2)}) collective-permute-start(bf16[3,2,64,128]{3,2,1,0:T(8,128)(2,1)S(1)} %get-tuple-element.43), channel_id=1, source_target_pairs={{0,64},{1,2},{2,1},{3,4},{4,3},{5,6},{6,5},{7,8},{8,7},{9,10},{10,... | collective-permute-start | bytes 294920 | tf_op jit(solution)/shard_map/ppermute | solution.py:348
  5.6 9.1 %copy-start = (bf16[4,27,128,128]{3,2,1,0:T(8,128)(2,1)S(1)}, bf16[4,27,128,128]{3,2,1,0:T(8,128)(2,1)}, u32[]{:S(2)}) copy-start(bf16[4,27,128,128]{3,2,1,0:T(8,128)(2,1)} %param.14) | copy-start | bytes 10616836
  12.1 4.1 %collective-permute-start.6 = (bf16[2,64,128]{2,1,0:T(8,128)(2,1)S(1)}, bf16[2,64,128]{2,1,0:T(8,128)(2,1)S(1)}, u32[]{:S(2)}, u32[]{:S(2)}) collective-permute-start(bf16[2,64,128]{2,1,0:T(8,128)(2,1)S(1)} %get-tuple-element.52), channel_id=1, source_target_pairs={{0,64},{1,65},{2,66},{3,67},{4,68},{5,69},{6,70},{7,71},{8,72},{9,... | collective-permute-start | bytes 98312 | tf_op jit(solution)/shard_map/ppermute | solution.py:348
  12.2 4.0 %collective-permute-start.7 = (bf16[2,64,128]{2,1,0:T(8,128)(2,1)S(1)}, bf16[2,64,128]{2,1,0:T(8,128)(2,1)S(1)}, u32[]{:S(2)}, u32[]{:S(2)}) collective-permute-start(bf16[2,64,128]{2,1,0:T(8,128)(2,1)S(1)} %get-tuple-element.53), channel_id=1, source_target_pairs={{0,1},{1,0},{2,3},{3,2},{4,5},{5,4},{6,7},{7,6},{8,9},{9,8},{10,11... | collective-permute-start | bytes 98312 | tf_op jit(solution)/shard_map/ppermute | solution.py:348
  12.7 3.5 %collective-permute-start.4 = (bf16[3,2,64,128]{3,2,1,0:T(8,128)(2,1)S(1)}, bf16[3,2,64,128]{3,2,1,0:T(8,128)(2,1)S(1)}, u32[]{:S(2)}, u32[]{:S(2)}) collective-permute-start(bf16[3,2,64,128]{3,2,1,0:T(8,128)(2,1)S(1)} %get-tuple-element.50), channel_id=1, source_target_pairs={{0,1},{1,0},{2,3},{3,2},{4,5},{5,4},{6,7},{7,6},{8,9},{9,8},{10,11... | collective-permute-start | bytes 294920 | tf_op jit(solution)/shard_map/ppermute | solution.py:348
  13.4 4.2 %collective-permute-start.5 = (bf16[3,2,64,128]{3,2,1,0:T(8,128)(2,1)S(1)}, bf16[3,2,64,128]{3,2,1,0:T(8,128)(2,1)S(1)}, u32[]{:S(2)}, u32[]{:S(2)}) collective-permute-start(bf16[3,2,64,128]{3,2,1,0:T(8,128)(2,1)S(1)} %get-tuple-element.51), channel_id=1, source_target_pairs={{0,64},{1,2},{2,1},{3,4},{4,3},{5,6},{6,5},{7,8},{8,7},{9,10},{10,... | collective-permute-start | bytes 294920 | tf_op jit(solution)/shard_map/ppermute | solution.py:348
  14.7 2.9 %copy-start.1 = (bf16[2,512,128]{2,1,0:T(8,128)(2,1)S(1)}, bf16[2,512,128]{2,1,0:T(8,128)(2,1)}, u32[]{:S(2)}) copy-start(bf16[2,512,128]{2,1,0:T(8,128)(2,1)} %rest_0_.3) | copy-start | bytes 786436
  20.0 4.7 %collective-permute-start.10 = (bf16[2,64,128]{2,1,0:T(8,128)(2,1)S(1)}, bf16[2,64,128]{2,1,0:T(8,128)(2,1)S(1)}, u32[]{:S(2)}, u32[]{:S(2)}) collective-permute-start(bf16[2,64,128]{2,1,0:T(8,128)(2,1)S(1)} %get-tuple-element.59), channel_id=1, source_target_pairs={{0,64},{1,65},{2,66},{3,67},{4,68},{5,69},{6,70},{7,71},{8,72},{9,... | collective-permute-start | bytes 98312 | tf_op jit(solution)/shard_map/ppermute | solution.py:348
  21.2 3.5 %collective-permute-start.11 = (bf16[2,64,128]{2,1,0:T(8,128)(2,1)S(1)}, bf16[2,64,128]{2,1,0:T(8,128)(2,1)S(1)}, u32[]{:S(2)}, u32[]{:S(2)}) collective-permute-start(bf16[2,64,128]{2,1,0:T(8,128)(2,1)S(1)} %get-tuple-element.60), channel_id=1, source_target_pairs={{0,1},{1,0},{2,3},{3,2},{4,5},{5,4},{6,7},{7,6},{8,9},{9,8},{10,11... | collective-permute-start | bytes 98312 | tf_op jit(solution)/shard_map/ppermute | solution.py:348
  21.5 3.2 %collective-permute-start.8 = (bf16[3,2,64,128]{3,2,1,0:T(8,128)(2,1)S(1)}, bf16[3,2,64,128]{3,2,1,0:T(8,128)(2,1)S(1)}, u32[]{:S(2)}, u32[]{:S(2)}) collective-permute-start(bf16[3,2,64,128]{3,2,1,0:T(8,128)(2,1)S(1)} %get-tuple-element.57), channel_id=1, source_target_pairs={{0,1},{1,0},{2,3},{3,2},{4,5},{5,4},{6,7},{7,6},{8,9},{9,8},{10,11... | collective-permute-start | bytes 294920 | tf_op jit(solution)/shard_map/ppermute | solution.py:348
  22.7 4.2 %collective-permute-start.9 = (bf16[3,2,64,128]{3,2,1,0:T(8,128)(2,1)S(1)}, bf16[3,2,64,128]{3,2,1,0:T(8,128)(2,1)S(1)}, u32[]{:S(2)}, u32[]{:S(2)}) collective-permute-start(bf16[3,2,64,128]{3,2,1,0:T(8,128)(2,1)S(1)} %get-tuple-element.58), channel_id=1, source_target_pairs={{0,64},{1,2},{2,1},{3,4},{4,3},{5,6},{6,5},{7,8},{8,7},{9,10},{10,... | collective-permute-start | bytes 294920 | tf_op jit(solution)/shard_map/ppermute | solution.py:348
  29.1 3.9 %collective-permute-start.14 = (bf16[2,64,128]{2,1,0:T(8,128)(2,1)S(1)}, bf16[2,64,128]{2,1,0:T(8,128)(2,1)S(1)}, u32[]{:S(2)}, u32[]{:S(2)}) collective-permute-start(bf16[2,64,128]{2,1,0:T(8,128)(2,1)S(1)} %get-tuple-element.66), channel_id=1, source_target_pairs={{0,64},{1,65},{2,66},{3,67},{4,68},{5,69},{6,70},{7,71},{8,72},{9,... | collective-permute-start | bytes 98312 | tf_op jit(solution)/shard_map/ppermute | solution.py:348
  29.2 3.8 %collective-permute-start.15 = (bf16[2,64,128]{2,1,0:T(8,128)(2,1)S(1)}, bf16[2,64,128]{2,1,0:T(8,128)(2,1)S(1)}, u32[]{:S(2)}, u32[]{:S(2)}) collective-permute-start(bf16[2,64,128]{2,1,0:T(8,128)(2,1)S(1)} %get-tuple-element.67), channel_id=1, source_target_pairs={{0,1},{1,0},{2,3},{3,2},{4,5},{5,4},{6,7},{7,6},{8,9},{9,8},{10,11... | collective-permute-start | bytes 98312 | tf_op jit(solution)/shard_map/ppermute | solution.py:348
  30.6 2.4 %collective-permute-start.12 = (bf16[3,2,64,128]{3,2,1,0:T(8,128)(2,1)S(1)}, bf16[3,2,64,128]{3,2,1,0:T(8,128)(2,1)S(1)}, u32[]{:S(2)}, u32[]{:S(2)}) collective-permute-start(bf16[3,2,64,128]{3,2,1,0:T(8,128)(2,1)S(1)} %get-tuple-element.64), channel_id=1, source_target_pairs={{0,1},{1,0},{2,3},{3,2},{4,5},{5,4},{6,7},{7,6},{8,9},{9,8},{10,11... | collective-permute-start | bytes 294920 | tf_op jit(solution)/shard_map/ppermute | solution.py:348
  31.5 4.2 %collective-permute-start.13 = (bf16[3,2,64,128]{3,2,1,0:T(8,128)(2,1)S(1)}, bf16[3,2,64,128]{3,2,1,0:T(8,128)(2,1)S(1)}, u32[]{:S(2)}, u32[]{:S(2)}) collective-permute-start(bf16[3,2,64,128]{3,2,1,0:T(8,128)(2,1)S(1)} %get-tuple-element.65), channel_id=1, source_target_pairs={{0,64},{1,2},{2,1},{3,4},{4,3},{5,6},{6,5},{7,8},{8,7},{9,10},{10,... | collective-permute-start | bytes 294920 | tf_op jit(solution)/shard_map/ppermute | solution.py:348
  37.6 66.0 %copy-start.2 = (bf16[128,512]{1,0:T(8,128)(2,1)S(1)}, bf16[128,512]{1,0:T(8,128)(2,1)}, u32[]{:S(2)}) copy-start(bf16[128,512]{1,0:T(8,128)(2,1)} %up.1) | copy-start | bytes 393220
